TPU v7x, 32 devices: a whole 2x2x4 slice. The times are simulated.
32 devices in a mesh: dp: 4 (over y, core), fsdp: 8 (over z, x).
Axes of the slice: x: 2, y: 2, z: 4, core: 2. Of those that a mesh axis runs over, the one named last changes fastest.
Arguments:
- tokens: bfloat16 [32, 1024, 512], P(('dp', 'fsdp')), may hold values from -6 to 6
- cotangent: bfloat16 [32, 1024, 512], P(('dp', 'fsdp')), may hold values from -6 to 6
- dataset_ids: int32 [32], P(('dp', 'fsdp')), may hold values from 0 to 7
- query_counts: int32 [32], P(('dp', 'fsdp')), may hold values from 1 to 128
- learn_rate: float32 [1], replicated, may hold values from 0.0002762136 to 0.00082864077
- momentum_coef: float32 [1], replicated, may hold values from 0.4 to 0.6
- average_decay: float32 [1], replicated, may hold values from 0.2 to 0.95
- step_count: int32 [1], replicated, may hold values from 2 to 20
- attend_weight: float32 [2, 512, 1536], P(None, ('dp', 'fsdp')), may hold values from -0.25 to 0.25
- attend_momentum: float32 [2, 512, 1536], P(None, ('dp', 'fsdp')), may hold values from -112 to 112
- attend_average: float32 [2, 512, 1536], P(None, ('dp', 'fsdp')), may hold values from -0.25 to 0.25
- output_weight: float32 [2, 512, 512], P(None, ('dp', 'fsdp')), may hold values from -1.5 to 1.5
- output_momentum: float32 [2, 512, 512], P(None, ('dp', 'fsdp')), may hold values from -20 to 20
- output_average: float32 [2, 512, 512], P(None, ('dp', 'fsdp')), may hold values from -1.5 to 1.5
- expand_weight: float32 [2, 512, 1024], P(None, ('dp', 'fsdp')), may hold values from -0.25 to 0.25
- expand_momentum: float32 [2, 512, 1024], P(None, ('dp', 'fsdp')), may hold values from -320 to 320
- expand_average: float32 [2, 512, 1024], P(None, ('dp', 'fsdp')), may hold values from -0.25 to 0.25
- shrink_weight: float32 [2, 1024, 512], P(None, ('dp', 'fsdp')), may hold values from -0.1875 to 0.1875
- shrink_momentum: float32 [2, 1024, 512], P(None, ('dp', 'fsdp')), may hold values from -320 to 320
- shrink_average: float32 [2, 1024, 512], P(None, ('dp', 'fsdp')), may hold values from -0.1875 to 0.1875
- norm_gains: float32 [2, 2, 512], P(None, None, ('dp', 'fsdp')), may hold values from 0.5 to 1.5
- gains_momentum: float32 [2, 2, 512], P(None, None, ('dp', 'fsdp')), may hold values from -320 to 320
- gains_average: float32 [2, 2, 512], P(None, None, ('dp', 'fsdp')), may hold values from 0.5 to 1.5
- bias_rows: float32 [2, 8, 512], P(None, None, ('dp', 'fsdp')), may hold values from -3 to 3
- bias_momentum: float32 [2, 8, 512], P(None, None, ('dp', 'fsdp')), may hold values from -320 to 320
- bias_average: float32 [2, 8, 512], P(None, None, ('dp', 'fsdp')), may hold values from -3 to 3
Outputs:
- layer_out: bfloat16 [32, 1024, 512], P(('dp', 'fsdp'))
- input_grad: float32 [32, 1024, 512], P(('dp', 'fsdp'))
- attend_velocity: float32 [2, 512, 1536], P(None, ('dp', 'fsdp'))
- attend_smoothed: float32 [2, 512, 1536], P(None, ('dp', 'fsdp'))
- attend_master: float32 [2, 512, 1536], P(None, ('dp', 'fsdp'))
- attend_copy: bfloat16 [2, 512, 1536], P(None, ('dp', 'fsdp'))
- output_velocity: float32 [2, 512, 512], P(None, ('dp', 'fsdp'))
- output_smoothed: float32 [2, 512, 512], P(None, ('dp', 'fsdp'))
- output_master: float32 [2, 512, 512], P(None, ('dp', 'fsdp'))
- output_copy: bfloat16 [2, 512, 512], P(None, ('dp', 'fsdp'))
- expand_velocity: float32 [2, 512, 1024], P(None, ('dp', 'fsdp'))
- expand_smoothed: float32 [2, 512, 1024], P(None, ('dp', 'fsdp'))
- expand_master: float32 [2, 512, 1024], P(None, ('dp', 'fsdp'))
- expand_copy: bfloat16 [2, 512, 1024], P(None, ('dp', 'fsdp'))
- shrink_velocity: float32 [2, 1024, 512], P(None, ('dp', 'fsdp'))
- shrink_smoothed: float32 [2, 1024, 512], P(None, ('dp', 'fsdp'))
- shrink_master: float32 [2, 1024, 512], P(None, ('dp', 'fsdp'))
- shrink_copy: bfloat16 [2, 1024, 512], P(None, ('dp', 'fsdp'))
- gains_velocity: float32 [2, 2, 512], P(None, None, ('dp', 'fsdp'))
- gains_smoothed: float32 [2, 2, 512], P(None, None, ('dp', 'fsdp'))
- gains_master: float32 [2, 2, 512], P(None, None, ('dp', 'fsdp'))
- gains_copy: bfloat16 [2, 2, 512], P(None, None, ('dp', 'fsdp'))
- bias_velocity: float32 [2, 8, 512], P(None, None, ('dp', 'fsdp'))
- bias_smoothed: float32 [2, 8, 512], P(None, None, ('dp', 'fsdp'))
- bias_master: float32 [2, 8, 512], P(None, None, ('dp', 'fsdp'))
- bias_copy: bfloat16 [2, 8, 512], P(None, None, ('dp', 'fsdp'))
All inputs are finite; a program needn't handle non-finite values.
Results may differ from a plain program's by a relative error of at most 0.02.
The roundings to bfloat16 on the way count: a program that leaves them out, or rounds other values in their place, can miss the bound.
Values may be sent and summed in bfloat16 or wider, within the bound.
No kernel may reach another device: no remote copies, remote signals or barrier semaphores. Data moves between devices by JAX's collectives and lax.ppermute only.
A program may use at most 192 MiB of HBM per device.

v0:
```python
import jax
import jax.numpy as jnp
from jax import lax
from jax.sharding import PartitionSpec as P

HEADS = 4
CTX = 896
NDS = 8


EPS = 1e-05


def norm_rows(summed, gain, shift):
    row_mean = jnp.mean(summed, axis=-1, keepdims=True)
    centred = summed - row_mean
    inv_std = lax.rsqrt(jnp.mean(centred * centred, axis=-1, keepdims=True) + EPS)
    unit_rows = centred * inv_std
    return (unit_rows * gain + shift, unit_rows, inv_std)


def norm_back(grad_rows, unit_rows, inv_std, gain):
    scaled = grad_rows * gain
    return inv_std * (
        scaled
        - jnp.mean(scaled, axis=-1, keepdims=True)
        - unit_rows * jnp.mean(scaled * unit_rows, axis=-1, keepdims=True)
    )


def gelu_slope(hidden):
    normal_cdf = 0.5 * (1.0 + jax.scipy.special.erf(hidden * 0.7071067811865476))
    normal_pdf = jnp.exp(-0.5 * hidden * hidden) * 0.3989422804014327
    return normal_cdf + hidden * normal_pdf


def attend_one(pieces):
    queries, key_rows, value_rows = pieces
    factor = queries.shape[-1] ** (-0.5)
    scaled = (
        jnp.einsum("qhe,khe->hqk", queries, key_rows, preferred_element_type=jnp.float32) * factor
    )
    row_top = jnp.max(scaled, axis=-1, keepdims=True)
    log_total = row_top + jnp.log(jnp.sum(jnp.exp(scaled - row_top), axis=-1, keepdims=True))
    softmax_low = jnp.exp(scaled - log_total).astype(jnp.bfloat16)
    mixed_sum = jnp.einsum(
        "hqk,khe->qhe", softmax_low, value_rows, preferred_element_type=jnp.float32
    )
    return (mixed_sum, log_total)


def attend_back(pieces):
    queries, key_rows, value_rows, log_total, grad_mixed = pieces
    factor = queries.shape[-1] ** (-0.5)
    scaled = (
        jnp.einsum("qhe,khe->hqk", queries, key_rows, preferred_element_type=jnp.float32) * factor
    )
    softmax_rows = jnp.exp(scaled - log_total)
    softmax_low = softmax_rows.astype(jnp.bfloat16)
    grad_values = jnp.einsum(
        "hqk,qhe->khe", softmax_low, grad_mixed, preferred_element_type=jnp.float32
    )
    grad_probs = jnp.einsum(
        "qhe,khe->hqk", grad_mixed, value_rows, preferred_element_type=jnp.float32
    )
    grad_scores = (
        factor
        * softmax_rows
        * (grad_probs - jnp.sum(softmax_rows * grad_probs, axis=-1, keepdims=True))
    ).astype(jnp.bfloat16)
    grad_query = jnp.einsum(
        "hqk,khe->qhe", grad_scores, key_rows, preferred_element_type=jnp.float32
    )
    grad_keys = jnp.einsum("hqk,qhe->khe", grad_scores, queries, preferred_element_type=jnp.float32)
    return (grad_query, grad_keys, grad_values)


def split_heads(joint_low, model_width):
    head_size = model_width // HEADS
    batch_rows = joint_low.shape[0]
    slot_rows = joint_low.shape[1]
    queries = joint_low[:, :, :model_width].reshape(batch_rows, slot_rows, HEADS, head_size)
    key_rows = joint_low[:, :CTX, model_width : 2 * model_width].reshape(
        batch_rows, CTX, HEADS, head_size
    )
    value_rows = joint_low[:, :CTX, 2 * model_width :].reshape(batch_rows, CTX, HEADS, head_size)
    return (queries, key_rows, value_rows)


def layer_forward(inputs_low, weights):
    attend_w, output_w, expand_w, shrink_w, gain_rows, bias_table = weights
    model_width = attend_w.shape[0]
    gain_vals = gain_rows.astype(jnp.float32)
    biases = bias_table.astype(jnp.float32)
    zeros_row = jnp.zeros((model_width,), jnp.float32)
    joint_sum = jnp.dot(inputs_low, attend_w, preferred_element_type=jnp.float32) + jnp.concatenate(
        [biases[0], zeros_row, biases[1]]
    )
    joint_low = joint_sum.astype(jnp.bfloat16)
    queries, key_rows, value_rows = split_heads(joint_low, model_width)
    mixed_sum, log_total = lax.map(attend_one, (queries, key_rows, value_rows))
    mixed_low = mixed_sum.reshape(inputs_low.shape[0], inputs_low.shape[1], model_width).astype(
        jnp.bfloat16
    )
    attn_out = jnp.dot(mixed_low, output_w, preferred_element_type=jnp.float32) + biases[2]
    first_norm, unit_one, inv_one = norm_rows(
        inputs_low.astype(jnp.float32) + attn_out, gain_vals[0], biases[4]
    )
    first_low = first_norm.astype(jnp.bfloat16)
    hidden = jnp.dot(first_low, expand_w, preferred_element_type=jnp.float32) + biases[6:].reshape(
        -1
    )
    act_low = jax.nn.gelu(hidden, approximate=False).astype(jnp.bfloat16)
    branch = jnp.dot(act_low, shrink_w, preferred_element_type=jnp.float32) + biases[3]
    result, unit_two, inv_two = norm_rows(first_norm + branch, gain_vals[1], biases[5])
    kept_values = (
        queries,
        key_rows,
        value_rows,
        log_total,
        mixed_low,
        unit_one,
        inv_one,
        first_low,
        hidden,
        act_low,
        unit_two,
        inv_two,
    )
    return (result, kept_values)


def layer_backward(inputs_low, weights, grad_out):
    attend_w, output_w, expand_w, shrink_w, gain_rows, bias_table = weights
    model_width = attend_w.shape[0]
    gain_vals = gain_rows.astype(jnp.float32)
    unused_result, kept_values = layer_forward(inputs_low, weights)
    (
        queries,
        key_rows,
        value_rows,
        log_total,
        mixed_low,
        unit_one,
        inv_one,
        first_low,
        hidden,
        act_low,
        unit_two,
        inv_two,
    ) = kept_values
    batch_rows = inputs_low.shape[0]
    slot_rows = inputs_low.shape[1]
    grad_two = norm_back(grad_out, unit_two, inv_two, gain_vals[1])
    gain_two = jnp.sum(grad_out * unit_two, axis=(0, 1))
    shift_two = jnp.sum(grad_out, axis=(0, 1))
    branch_low = grad_two.astype(jnp.bfloat16)
    grad_shrink = jnp.einsum("nsf,nsd->fd", act_low, branch_low, preferred_element_type=jnp.float32)
    bias_branch = jnp.sum(branch_low.astype(jnp.float32), axis=(0, 1))
    grad_hidden = (
        jnp.einsum("nsd,fd->nsf", branch_low, shrink_w, preferred_element_type=jnp.float32)
        * gelu_slope(hidden)
    ).astype(jnp.bfloat16)
    grad_expand = jnp.einsum(
        "nsd,nsf->df", first_low, grad_hidden, preferred_element_type=jnp.float32
    )
    bias_hidden = jnp.sum(grad_hidden.astype(jnp.float32), axis=(0, 1))
    grad_first = grad_two + jnp.einsum(
        "nsf,df->nsd", grad_hidden, expand_w, preferred_element_type=jnp.float32
    )
    grad_one = norm_back(grad_first, unit_one, inv_one, gain_vals[0])
    gain_one = jnp.sum(grad_first * unit_one, axis=(0, 1))
    shift_one = jnp.sum(grad_first, axis=(0, 1))
    attn_low = grad_one.astype(jnp.bfloat16)
    grad_output = jnp.einsum("nsd,nse->de", mixed_low, attn_low, preferred_element_type=jnp.float32)
    bias_attn = jnp.sum(attn_low.astype(jnp.float32), axis=(0, 1))
    grad_mixed = jnp.einsum(
        "nse,de->nsd", attn_low, output_w, preferred_element_type=jnp.float32
    ).astype(jnp.bfloat16)
    grad_heads = grad_mixed.reshape(batch_rows, slot_rows, HEADS, model_width // HEADS)
    grad_query, grad_keys, grad_values = lax.map(
        attend_back, (queries, key_rows, value_rows, log_total, grad_heads)
    )
    rim_pad = ((0, 0), (0, slot_rows - CTX), (0, 0))
    keys_full = jnp.pad(grad_keys.reshape(batch_rows, CTX, model_width), rim_pad)
    values_full = jnp.pad(grad_values.reshape(batch_rows, CTX, model_width), rim_pad)
    grad_joint = jnp.concatenate(
        [grad_query.reshape(batch_rows, slot_rows, model_width), keys_full, values_full], axis=-1
    ).astype(jnp.bfloat16)
    grad_attend = jnp.einsum(
        "nsd,nsj->dj", inputs_low, grad_joint, preferred_element_type=jnp.float32
    )
    joint_bias = jnp.sum(grad_joint.astype(jnp.float32), axis=(0, 1))
    grad_input = grad_one + jnp.einsum(
        "nsj,dj->nsd", grad_joint, attend_w, preferred_element_type=jnp.float32
    )
    grad_gains = jnp.stack([gain_one, gain_two])
    grad_biases = jnp.concatenate(
        [
            jnp.stack(
                [
                    joint_bias[:model_width],
                    joint_bias[2 * model_width :],
                    bias_attn,
                    bias_branch,
                    shift_one,
                    shift_two,
                ]
            ),
            bias_hidden.reshape(-1, model_width),
        ],
        axis=0,
    )
    return (
        (grad_attend, grad_output, grad_expand, grad_shrink, grad_gains, grad_biases),
        grad_input,
    )


def collect(masters, layer_index):
    pieces = tuple((master[layer_index].astype(jnp.bfloat16) for master in masters))
    inner_part = (
        lax.all_gather(pieces[0], "fsdp", axis=0, tiled=True),
        lax.all_gather(pieces[1], "fsdp", axis=0, tiled=True),
        lax.all_gather(pieces[2], "fsdp", axis=0, tiled=True),
        lax.all_gather(pieces[3], "fsdp", axis=0, tiled=True),
        lax.all_gather(pieces[4], "fsdp", axis=1, tiled=True),
        lax.all_gather(pieces[5], "fsdp", axis=1, tiled=True),
    )
    return (
        lax.all_gather(inner_part[0], "dp", axis=0, tiled=True),
        lax.all_gather(inner_part[1], "dp", axis=0, tiled=True),
        lax.all_gather(inner_part[2], "dp", axis=0, tiled=True),
        lax.all_gather(inner_part[3], "dp", axis=0, tiled=True),
        lax.all_gather(inner_part[4], "dp", axis=1, tiled=True),
        lax.all_gather(inner_part[5], "dp", axis=1, tiled=True),
    )


def settle(local_grads):
    outer_part = (
        lax.psum_scatter(
            local_grads[0].astype(jnp.bfloat16), "dp", scatter_dimension=0, tiled=True
        ).astype(jnp.float32),
        lax.psum_scatter(
            local_grads[1].astype(jnp.bfloat16), "dp", scatter_dimension=0, tiled=True
        ).astype(jnp.float32),
        lax.psum_scatter(
            local_grads[2].astype(jnp.bfloat16), "dp", scatter_dimension=0, tiled=True
        ).astype(jnp.float32),
        lax.psum_scatter(
            local_grads[3].astype(jnp.bfloat16), "dp", scatter_dimension=0, tiled=True
        ).astype(jnp.float32),
        lax.psum_scatter(
            local_grads[4].astype(jnp.bfloat16), "dp", scatter_dimension=1, tiled=True
        ).astype(jnp.float32),
        lax.psum_scatter(
            local_grads[5].astype(jnp.bfloat16), "dp", scatter_dimension=1, tiled=True
        ).astype(jnp.float32),
    )
    return (
        lax.psum_scatter(
            outer_part[0].astype(jnp.bfloat16), "fsdp", scatter_dimension=0, tiled=True
        ).astype(jnp.float32),
        lax.psum_scatter(
            outer_part[1].astype(jnp.bfloat16), "fsdp", scatter_dimension=0, tiled=True
        ).astype(jnp.float32),
        lax.psum_scatter(
            outer_part[2].astype(jnp.bfloat16), "fsdp", scatter_dimension=0, tiled=True
        ).astype(jnp.float32),
        lax.psum_scatter(
            outer_part[3].astype(jnp.bfloat16), "fsdp", scatter_dimension=0, tiled=True
        ).astype(jnp.float32),
        lax.psum_scatter(
            outer_part[4].astype(jnp.bfloat16), "fsdp", scatter_dimension=1, tiled=True
        ).astype(jnp.float32),
        lax.psum_scatter(
            outer_part[5].astype(jnp.bfloat16), "fsdp", scatter_dimension=1, tiled=True
        ).astype(jnp.float32),
    )


def advance(master, moment, average, grad, momentum, step_rate, decay_now):
    new_moment = momentum * moment + grad
    new_master = master - step_rate * (grad + momentum * new_moment)
    new_average = decay_now * average + (1.0 - decay_now) * new_master
    return (new_moment, new_average, new_master, new_master.astype(jnp.bfloat16))


def shards(
    tokens,
    cotangent,
    dataset_ids,
    query_counts,
    learn_rate,
    momentum_coef,
    average_decay,
    step_count,
    attend_weight,
    attend_momentum,
    attend_average,
    output_weight,
    output_momentum,
    output_average,
    expand_weight,
    expand_momentum,
    expand_average,
    shrink_weight,
    shrink_momentum,
    shrink_average,
    norm_gains,
    gains_momentum,
    gains_average,
    bias_rows,
    bias_momentum,
    bias_average,
):
    masters = (attend_weight, output_weight, expand_weight, shrink_weight, norm_gains, bias_rows)
    moments = (
        attend_momentum,
        output_momentum,
        expand_momentum,
        shrink_momentum,
        gains_momentum,
        bias_momentum,
    )
    averages = (
        attend_average,
        output_average,
        expand_average,
        shrink_average,
        gains_average,
        bias_average,
    )
    layers = attend_weight.shape[0]
    onehot = (dataset_ids[:, None] == jnp.arange(NDS, dtype=jnp.int32)[None, :]).astype(jnp.float32)
    counts = lax.psum(jnp.sum(onehot, axis=0), ("dp", "fsdp"))
    own_count = jnp.sum(onehot * counts[None, :], axis=1)
    row_weight = jnp.sum(counts) / (NDS * own_count)
    positions = jnp.arange(tokens.shape[1], dtype=jnp.int32)
    live_rows = (
        (positions[None, :] < CTX) | (positions[None, :] - CTX < query_counts[:, None])
    ).astype(jnp.float32)
    effective = cotangent.astype(jnp.float32) * (live_rows * row_weight[:, None])[:, :, None]
    current = tokens
    inputs_kept = []
    gathered_kept = []
    for layer_index in range(layers):
        weights = collect(masters, layer_index)
        gathered_kept.append(weights)
        inputs_kept.append(current)
        result, unused_kept = layer_forward(current, weights)
        current = result.astype(jnp.bfloat16)
    grad_rows = effective
    shard_grads = [None] * layers
    for layer_index in reversed(range(layers)):
        weights = collect(masters, layer_index)
        local_grads, grad_rows = layer_backward(inputs_kept[layer_index], weights, grad_rows)
        shard_grads[layer_index] = settle(local_grads)
    step_value = step_count[0].astype(jnp.float32)
    decay_now = average_decay[0] * (1.0 + step_value) / (4.0 + step_value)
    outputs = [current, grad_rows]
    for group_index in range(6):
        stacked = jnp.stack(
            [shard_grads[layer_index][group_index] for layer_index in range(layers)]
        )
        outputs.extend(
            advance(
                masters[group_index],
                moments[group_index],
                averages[group_index],
                stacked,
                momentum_coef[0],
                learn_rate[0],
                decay_now,
            )
        )
    return tuple(outputs)


def solution(mesh):
    return jax.shard_map(
        shards,
        mesh=mesh,
        in_specs=(
            P(("dp", "fsdp"), None, None),
            P(("dp", "fsdp"), None, None),
            P(("dp", "fsdp")),
            P(("dp", "fsdp")),
            P(),
            P(),
            P(),
            P(),
            P(None, ("dp", "fsdp"), None),
            P(None, ("dp", "fsdp"), None),
            P(None, ("dp", "fsdp"), None),
            P(None, ("dp", "fsdp"), None),
            P(None, ("dp", "fsdp"), None),
            P(None, ("dp", "fsdp"), None),
            P(None, ("dp", "fsdp"), None),
            P(None, ("dp", "fsdp"), None),
            P(None, ("dp", "fsdp"), None),
            P(None, ("dp", "fsdp"), None),
            P(None, ("dp", "fsdp"), None),
            P(None, ("dp", "fsdp"), None),
            P(None, None, ("dp", "fsdp")),
            P(None, None, ("dp", "fsdp")),
            P(None, None, ("dp", "fsdp")),
            P(None, None, ("dp", "fsdp")),
            P(None, None, ("dp", "fsdp")),
            P(None, None, ("dp", "fsdp")),
        ),
        out_specs=(
            P(("dp", "fsdp"), None, None),
            P(("dp", "fsdp"), None, None),
            P(None, ("dp", "fsdp"), None),
            P(None, ("dp", "fsdp"), None),
            P(None, ("dp", "fsdp"), None),
            P(None, ("dp", "fsdp"), None),
            P(None, ("dp", "fsdp"), None),
            P(None, ("dp", "fsdp"), None),
            P(None, ("dp", "fsdp"), None),
            P(None, ("dp", "fsdp"), None),
            P(None, ("dp", "fsdp"), None),
            P(None, ("dp", "fsdp"), None),
            P(None, ("dp", "fsdp"), None),
            P(None, ("dp", "fsdp"), None),
            P(None, ("dp", "fsdp"), None),
            P(None, ("dp", "fsdp"), None),
            P(None, ("dp", "fsdp"), None),
            P(None, ("dp", "fsdp"), None),
            P(None, None, ("dp", "fsdp")),
            P(None, None, ("dp", "fsdp")),
            P(None, None, ("dp", "fsdp")),
            P(None, None, ("dp", "fsdp")),
            P(None, None, ("dp", "fsdp")),
            P(None, None, ("dp", "fsdp")),
            P(None, None, ("dp", "fsdp")),
            P(None, None, ("dp", "fsdp")),
        ),
        check_vma=False,
    )
```

profile of v0, /device:TPU:0, one launch (start us, length us, event | category | flops | bytes accessed | tf_op | source)
XLA Modules:
  0.0 1719.5 jit_solution(18441274299703874597)
XLA Ops:
  8.3 34.9 %all-gather = bf16[1,128,1536]{2,1,0:T(8,128)(2,1)} all-gather(bf16[1,16,1536]{2,1,0:T(8,128)(2,1)S(1)} %get-tuple-element.300), channel_id=2, replica_groups=mesh['dp'=4,'fsdp'=8] {'fsdp'}, dimensions={1}, use_global_device_ids=true | all-gather | bytes 442368 | tf_op jit(solution)/shard_map/all_gather | solution.py:223
  44.3 32.8 %all-gather.8 = bf16[1,128,1024]{2,1,0:T(8,128)(2,1)} all-gather(bf16[1,16,1024]{2,1,0:T(8,128)(2,1)S(1)} %get-tuple-element.303), channel_id=10, replica_groups=mesh['dp'=4,'fsdp'=8] {'fsdp'}, dimensions={1}, use_global_device_ids=true | all-gather | bytes 294912 | tf_op jit(solution)/shard_map/all_gather | solution.py:225
  78.1 32.8 %all-gather.10 = bf16[1,256,512]{2,1,0:T(8,128)(2,1)} all-gather(bf16[1,32,512]{2,1,0:T(8,128)(2,1)S(1)} %get-tuple-element.302), channel_id=12, replica_groups=mesh['dp'=4,'fsdp'=8] {'fsdp'}, dimensions={1}, use_global_device_ids=true | all-gather | bytes 294912 | tf_op jit(solution)/shard_map/all_gather | solution.py:226
  111.0 33.0 %all-gather.12 = bf16[1,128,1536]{2,1,0:T(8,128)(2,1)} all-gather(bf16[1,16,1536]{2,1,0:T(8,128)(2,1)S(1)} %get-tuple-element.299), channel_id=14, replica_groups=mesh['dp'=4,'fsdp'=8] {'fsdp'}, dimensions={1}, use_global_device_ids=true | all-gather | bytes 442368 | tf_op jit(solution)/shard_map/all_gather | solution.py:223
  144.0 32.8 %all-gather.20 = bf16[1,128,1024]{2,1,0:T(8,128)(2,1)} all-gather(bf16[1,16,1024]{2,1,0:T(8,128)(2,1)S(1)} %get-tuple-element.304), channel_id=22, replica_groups=mesh['dp'=4,'fsdp'=8] {'fsdp'}, dimensions={1}, use_global_device_ids=true | all-gather | bytes 294912 | tf_op jit(solution)/shard_map/all_gather | solution.py:225
  176.9 32.7 %all-gather.22 = bf16[1,256,512]{2,1,0:T(8,128)(2,1)} all-gather(bf16[1,32,512]{2,1,0:T(8,128)(2,1)S(1)} %get-tuple-element.301), channel_id=24, replica_groups=mesh['dp'=4,'fsdp'=8] {'fsdp'}, dimensions={1}, use_global_device_ids=true | all-gather | bytes 294912 | tf_op jit(solution)/shard_map/all_gather | solution.py:226
  209.8 30.5 %all-gather.14 = bf16[1,8,128]{1,0,2:T(2,128)(2,1)S(1)} all-gather(bf16[1,8,16]{1,0,2:T(2,128)(2,1)S(1)} %get-tuple-element.315), channel_id=16, replica_groups=mesh['dp'=4,'fsdp'=8] {'fsdp'}, dimensions={2}, use_global_device_ids=true | all-gather | bytes 2304 | tf_op jit(solution)/shard_map/all_gather | solution.py:228
  246.2 30.5 %all-gather.2 = bf16[1,8,128]{1,0,2:T(2,128)(2,1)S(1)} all-gather(bf16[1,8,16]{1,0,2:T(2,128)(2,1)S(1)} %get-tuple-element.316), channel_id=4, replica_groups=mesh['dp'=4,'fsdp'=8] {'fsdp'}, dimensions={2}, use_global_device_ids=true | all-gather | bytes 2304 | tf_op jit(solution)/shard_map/all_gather | solution.py:228
  283.9 39.7 %psum.7 = f32[8]{0:T(128)S(1)} all-reduce(f32[8]{0:T(128)S(1)} %compare_convert_fusion), channel_id=1, replica_groups=mesh['dp'=4,'fsdp'=8] {'dp','fsdp'}, use_global_device_ids=true, to_apply=%region_12.13 | all-reduce | flops 8 | bytes 64 | tf_op jit(solution)/shard_map/psum | solution.py:337
  323.8 30.5 %all-gather.18 = bf16[1,2,128]{1,0,2:T(2,128)(2,1)S(1)} all-gather(bf16[1,2,16]{1,0,2:T(2,128)(2,1)S(1)} %get-tuple-element.313), channel_id=20, replica_groups=mesh['dp'=4,'fsdp'=8] {'fsdp'}, dimensions={2}, use_global_device_ids=true | all-gather | bytes 576 | tf_op jit(solution)/shard_map/all_gather | solution.py:227
  360.9 30.5 %all-gather.6 = bf16[1,2,128]{1,0,2:T(2,128)(2,1)S(1)} all-gather(bf16[1,2,16]{1,0,2:T(2,128)(2,1)S(1)} %get-tuple-element.314), channel_id=8, replica_groups=mesh['dp'=4,'fsdp'=8] {'fsdp'}, dimensions={2}, use_global_device_ids=true | all-gather | bytes 576 | tf_op jit(solution)/shard_map/all_gather | solution.py:227
  427.7 30.5 %all-gather.4 = bf16[1,128,512]{2,1,0:T(8,128)(2,1)S(1)} all-gather(bf16[1,16,512]{2,1,0:T(8,128)(2,1)S(1)} %get-tuple-element.306), channel_id=6, replica_groups=mesh['dp'=4,'fsdp'=8] {'fsdp'}, dimensions={1}, use_global_device_ids=true | all-gather | bytes 147456 | tf_op jit(solution)/shard_map/all_gather | solution.py:224
  915.7 47.0 %reduce-scatter.87.cloned.1.call-done = bf16[16,2]{1,0:T(8,128)(2,1)} async-done(((bf16[128,2]{1,0:T(8,128)(2,1)}), bf16[16,2]{1,0:T(8,128)(2,1)}) %reduce-scatter.87.cloned.1.call-update) | async-done | bytes 80
  963.5 56.1 %reduce-scatter.83.cloned.1.call-done = bf16[16,2]{1,0:T(8,128)(2,1)} async-done(((bf16[128,2]{1,0:T(8,128)(2,1)}), bf16[16,2]{1,0:T(8,128)(2,1)}) %reduce-scatter.83.cloned.1.call-update) | async-done | bytes 80
  1021.5 55.0 %reduce-scatter.95.cloned.1.call-done = bf16[16,8]{1,0:T(8,128)(2,1)} async-done(((bf16[128,8]{1,0:T(8,128)(2,1)}), bf16[16,8]{1,0:T(8,128)(2,1)}) %reduce-scatter.95.cloned.1.call-update) | async-done | bytes 272
  1077.3 56.1 %reduce-scatter.91.cloned.1.call-done = bf16[16,8]{1,0:T(8,128)(2,1)} async-done(((bf16[128,8]{1,0:T(8,128)(2,1)}), bf16[16,8]{1,0:T(8,128)(2,1)}) %reduce-scatter.91.cloned.1.call-update) | async-done | bytes 272
  1164.4 64.0 %reduce-scatter.55.cloned.1.call-done = bf16[16,512]{1,0:T(8,128)(2,1)} async-done(((bf16[128,512]{1,0:T(8,128)(2,1)}), bf16[16,512]{1,0:T(8,128)(2,1)}) %reduce-scatter.55.cloned.1.call-update) | async-done | bytes 16400 | tf_op jit(solution)/shard_map/reduce_scatter | solution.py:265
  1228.3 64.2 %reduce-scatter.51.cloned.1.call-done = bf16[16,512]{1,0:T(8,128)(2,1)} async-done(((bf16[128,512]{1,0:T(8,128)(2,1)}), bf16[16,512]{1,0:T(8,128)(2,1)}) %reduce-scatter.51.cloned.1.call-update) | async-done | bytes 16400 | tf_op jit(solution)/shard_map/reduce_scatter | solution.py:265
  1322.1 65.4 %reduce-scatter.63.cloned.1.call-done = bf16[16,1024]{1,0:T(8,128)(2,1)} async-done(((bf16[128,1024]{1,0:T(8,128)(2,1)}), bf16[16,1024]{1,0:T(8,128)(2,1)}) %reduce-scatter.63.cloned.1.call-update) | async-done | bytes 32784 | tf_op jit(solution)/shard_map/reduce_scatter | solution.py:268
  1387.5 64.3 %reduce-scatter.59.cloned.1.call-done = bf16[16,1024]{1,0:T(8,128)(2,1)} async-done(((bf16[128,1024]{1,0:T(8,128)(2,1)}), bf16[16,1024]{1,0:T(8,128)(2,1)}) %reduce-scatter.59.cloned.1.call-update) | async-done | bytes 32784 | tf_op jit(solution)/shard_map/reduce_scatter | solution.py:268
  1454.0 62.1 %reduce-scatter.71.cloned.1.call-done = bf16[32,512]{1,0:T(8,128)(2,1)} async-done(((bf16[256,512]{1,0:T(8,128)(2,1)}), bf16[32,512]{1,0:T(8,128)(2,1)}) %reduce-scatter.71.cloned.1.call-update) | async-done | bytes 32784 | tf_op jit(solution)/shard_map/reduce_scatter | solution.py:271
  1516.1 64.5 %reduce-scatter.67.cloned.1.call-done = bf16[32,512]{1,0:T(8,128)(2,1)} async-done(((bf16[256,512]{1,0:T(8,128)(2,1)}), bf16[32,512]{1,0:T(8,128)(2,1)}) %reduce-scatter.67.cloned.1.call-update) | async-done | bytes 32784 | tf_op jit(solution)/shard_map/reduce_scatter | solution.py:271
  1582.8 62.4 %reduce-scatter.79.cloned.1.call-done = bf16[16,1536]{1,0:T(8,128)(2,1)} async-done(((bf16[128,1536]{1,0:T(8,128)(2,1)}), bf16[16,1536]{1,0:T(8,128)(2,1)}) %reduce-scatter.79.cloned.1.call-update) | async-done | bytes 49168
  1646.4 63.2 %reduce-scatter.75.cloned.1.call-done = bf16[16,1536]{1,0:T(8,128)(2,1)} async-done(((bf16[128,1536]{1,0:T(8,128)(2,1)}), bf16[16,1536]{1,0:T(8,128)(2,1)}) %reduce-scatter.75.cloned.1.call-update) | async-done | bytes 49168
  (454 shorter events, 582.2 us)
Async XLA Ops:
  7.2 472.4 %all-gather.31.cloned.1.call-start = ((), (), s32[]{:S(2)}) async-start(), calls=%async_computation.36 | async-start | bytes 1966080 | tf_op jit(solution)/shard_map/all_gather | solution.py:231
  43.2 468.5 %all-gather.33.cloned.1.call-start = ((), (), s32[]{:S(2)}) async-start(), calls=%async_computation.37 | async-start | bytes 1310720 | tf_op jit(solution)/shard_map/all_gather | solution.py:233
  77.1 448.1 %all-gather.35.cloned.1.call-start = ((), (), s32[]{:S(2)}) async-start(), calls=%async_computation.38 | async-start | bytes 1310720 | tf_op jit(solution)/shard_map/all_gather | solution.py:234
  110.9 419.4 %all-gather.37.cloned.1.call-start = ((), (), s32[]{:S(2)}) async-start(), calls=%async_computation.39 | async-start | bytes 1966080 | tf_op jit(solution)/shard_map/all_gather | solution.py:231
  144.0 419.7 %all-gather.39.cloned.1.call-start = ((), (), s32[]{:S(2)}) async-start(), calls=%async_computation.40 | async-start | bytes 1310720 | tf_op jit(solution)/shard_map/all_gather | solution.py:233
  176.8 400.5 %all-gather.41.cloned.1.call-start = ((), (), s32[]{:S(2)}) async-start(), calls=%async_computation.41 | async-start | bytes 1310720 | tf_op jit(solution)/shard_map/all_gather | solution.py:234
  209.7 487.7 %reduce-scatter.85.cloned.1.call-start = ((), (), s32[]{:S(2)}) async-start(), calls=%async_computation.48 | async-start | bytes 163840
  683.7 166.9 %reduce-scatter.57.cloned.1.call-start = ((), (), s32[]{:S(2)}) async-start(), calls=%async_computation.28 | async-start | bytes 1310720 | tf_op jit(solution)/shard_map/reduce_scatter | solution.py:248
  688.3 189.4 %reduce-scatter.69.cloned.1.call-start = ((), (), s32[]{:S(2)}) async-start(), calls=%async_computation.34 | async-start | bytes 1310720 | tf_op jit(solution)/shard_map/reduce_scatter | solution.py:251
  692.5 212.4 %reduce-scatter.65.cloned.1.call-start = ((), (), s32[]{:S(2)}) async-start(), calls=%async_computation.32 | async-start | bytes 1310720 | tf_op jit(solution)/shard_map/reduce_scatter | solution.py:251
  697.3 265.4 %reduce-scatter.87.cloned.1.call-start = ((), (), s32[]{:S(2)}) async-start(), calls=%async_computation.49 | async-start | bytes 36864
  697.9 321.7 %reduce-scatter.83.cloned.1.call-start = ((), (), s32[]{:S(2)}) async-start(), calls=%async_computation.47 | async-start | bytes 36864
  702.7 373.9 %reduce-scatter.95.cloned.1.call-start = ((), (), s32[]{:S(2)}) async-start(), calls=%async_computation.53 | async-start | bytes 36864
  725.3 408.1 %reduce-scatter.91.cloned.1.call-start = ((), (), s32[]{:S(2)}) async-start(), calls=%async_computation.51 | async-start | bytes 36864
  747.8 415.2 %reduce-scatter.77.cloned.1.call-start = ((), (), s32[]{:S(2)}) async-start(), calls=%async_computation.44 | async-start | bytes 1966080
  753.1 475.3 %reduce-scatter.55.cloned.1.call-start = ((), (), s32[]{:S(2)}) async-start(), calls=%async_computation.27 | async-start | bytes 147456 | tf_op jit(solution)/shard_map/reduce_scatter | solution.py:265
  772.0 520.6 %reduce-scatter.51.cloned.1.call-start = ((), (), s32[]{:S(2)}) async-start(), calls=%async_computation.25 | async-start | bytes 147456 | tf_op jit(solution)/shard_map/reduce_scatter | solution.py:265
  796.1 526.0 %reduce-scatter.73.cloned.1.call-start = ((), (), s32[]{:S(2)}) async-start(), calls=%async_computation.42 | async-start | bytes 1966080
  804.0 583.5 %reduce-scatter.63.cloned.1.call-start = ((), (), s32[]{:S(2)}) async-start(), calls=%async_computation.31 | async-start | bytes 294912 | tf_op jit(solution)/shard_map/reduce_scatter | solution.py:268
  823.4 628.4 %reduce-scatter.59.cloned.1.call-start = ((), (), s32[]{:S(2)}) async-start(), calls=%async_computation.29 | async-start | bytes 294912 | tf_op jit(solution)/shard_map/reduce_scatter | solution.py:268
  850.5 665.6 %reduce-scatter.71.cloned.1.call-start = ((), (), s32[]{:S(2)}) async-start(), calls=%async_computation.35 | async-start | bytes 294912 | tf_op jit(solution)/shard_map/reduce_scatter | solution.py:271
  877.7 702.9 %reduce-scatter.67.cloned.1.call-start = ((), (), s32[]{:S(2)}) async-start(), calls=%async_computation.33 | async-start | bytes 294912 | tf_op jit(solution)/shard_map/reduce_scatter | solution.py:271
  904.9 740.3 %reduce-scatter.79.cloned.1.call-start = ((), (), s32[]{:S(2)}) async-start(), calls=%async_computation.45 | async-start | bytes 442368
  1163.1 546.6 %reduce-scatter.75.cloned.1.call-start = ((), (), s32[]{:S(2)}) async-start(), calls=%async_computation.43 | async-start | bytes 442368
  (104 other events, 13074.0 us)
Sparse Core Ops, SparseCore 0:
  43.3 20.5 all-gather.30
  144.1 20.6 all-gather.36
  683.0 19.6 reduce-scatter.80
  728.2 19.6 reduce-scatter.88
  750.3 21.6 reduce-scatter.52
  774.3 21.6 reduce-scatter.48
  798.6 24.7 reduce-scatter.60
  825.7 24.7 reduce-scatter.56
  852.9 24.7 reduce-scatter.68
  880.1 24.7 reduce-scatter.64
  907.9 54.7 reduce-scatter.86
  965.7 53.8 reduce-scatter.82
  1022.7 53.7 reduce-scatter.94
  1079.5 53.8 reduce-scatter.90
  1135.9 27.0 reduce-scatter.76
  1166.4 61.9 reduce-scatter.54
  1231.7 60.8 reduce-scatter.50
  1295.0 27.0 reduce-scatter.72
  1325.4 62.0 reduce-scatter.62
  1390.7 61.1 reduce-scatter.58
  1455.0 61.1 reduce-scatter.70
  1519.5 61.1 reduce-scatter.66
  1583.9 61.3 reduce-scatter.78
  1648.4 61.2 reduce-scatter.74
  (6 shorter events, 108.0 us)
where the time goes:
time: 1720 us
  waiting for transfers between devices  969 us (56%)
  blocking collectives  458 us (27%)
  matrix products  157 us (9%)
  other arithmetic  56.7 us (3%)
  local copies, waits for them, and re-layouts  55.4 us (3%)
  between operations  21.5 us (1%)
    unnamed x42, waiting for transfers between devices  447 us
    reduce_scatter x2, waiting for transfers between devices, settle(): lax.psum_scatter(outer_part[2].astype(jnp.bfloat16), 'fsdp', scatter_dime...  130 us
    reduce_scatter x2, waiting for transfers between devices, settle(): lax.psum_scatter(outer_part[1].astype(jnp.bfloat16), 'fsdp', scatter_dime...  128 us
    reduce_scatter x2, waiting for transfers between devices, settle(): lax.psum_scatter(outer_part[3].astype(jnp.bfloat16), 'fsdp', scatter_dime...  127 us
    all_gather x2, blocking collectives, collect(): lax.all_gather(pieces[0], 'fsdp', axis=0, tiled=True)  67.8 us
    all_gather x2, blocking collectives, collect(): lax.all_gather(pieces[2], 'fsdp', axis=0, tiled=True)  65.6 us
    all_gather x2, blocking collectives, collect(): lax.all_gather(pieces[3], 'fsdp', axis=0, tiled=True)  65.6 us
    all_gather x2, blocking collectives, collect(): lax.all_gather(pieces[5], 'fsdp', axis=1, tiled=True)  61.1 us
  transfers between devices with their start and end apart: 30, of which 23 were waited for; matrix products, arithmetic and copies ran while one was open for 10% of the time, Pallas kernels for 0%

commit v1 on v0

--- a/solution.py
+++ b/solution.py
@@ -1,6 +1,9 @@
 import jax
 import jax.numpy as jnp
+import numpy as np
 from jax import lax
+from jax.experimental import pallas as pl
+from jax.experimental.pallas import tpu as pltpu
 from jax.sharding import PartitionSpec as P
 
 HEADS = 4
@@ -217,68 +220,96 @@
     )
 
 
-def collect(masters, layer_index):
-    pieces = tuple((master[layer_index].astype(jnp.bfloat16) for master in masters))
-    inner_part = (
-        lax.all_gather(pieces[0], "fsdp", axis=0, tiled=True),
-        lax.all_gather(pieces[1], "fsdp", axis=0, tiled=True),
-        lax.all_gather(pieces[2], "fsdp", axis=0, tiled=True),
-        lax.all_gather(pieces[3], "fsdp", axis=0, tiled=True),
-        lax.all_gather(pieces[4], "fsdp", axis=1, tiled=True),
-        lax.all_gather(pieces[5], "fsdp", axis=1, tiled=True),
-    )
+class Route:
+    def __init__(self, steps, inner_size):
+        self.steps = steps
+        masks = [bit * inner_size if axis == "dp" else bit for axis, size, bit in steps]
+        self.count = 1 << len(steps)
+        self.offset = [
+            sum(mask for at, mask in enumerate(masks) if place >> at & 1)
+            for place in range(self.count)
+        ]
+
+    def swap(self, at, payload):
+        axis, size, bit = self.steps[at]
+        return lax.ppermute(payload, axis, [(one, one ^ bit) for one in range(size)])
+
+
+def routes(outer_size, inner_size):
+    outer = [("dp", outer_size, 1 << at) for at in reversed(range(outer_size.bit_length() - 1))]
+    inner = [("fsdp", inner_size, 1 << at) for at in reversed(range(inner_size.bit_length() - 1))]
+    first = inner + outer
+    second = inner[:-1] + outer[:-1] + inner[-1:] + outer[-1:]
+    return (Route(first, inner_size), Route(second, inner_size))
+
+
+def spread(route, block, shared=None):
+    rows, width = block.shape
+    for at in range(len(route.steps)):
+        held = block.shape[0]
+        payload = block if shared is None else jnp.concatenate([block, shared])
+        got = route.swap(at, payload)
+        block = jnp.concatenate([block, got[:held]])
+        if shared is not None:
+            shared = shared + got[held:]
+    return (block.reshape(route.count, rows, width), shared)
+
+
+def gather_sum(route, slots, shared=None):
+    count, rows, width = slots.shape
+    block = slots.reshape(count * rows, width)
+    for at in reversed(range(len(route.steps))):
+        half = block.shape[0] // 2
+        payload = block[half:] if shared is None else jnp.concatenate([block[half:], shared])
+        got = route.swap(at, payload)
+        block = (block[:half].astype(jnp.float32) + got[:half].astype(jnp.float32)).astype(
+            jnp.bfloat16
+        )
+        if shared is not None:
+            shared = (shared.astype(jnp.float32) + got[half:].astype(jnp.float32)).astype(
+                jnp.bfloat16
+            )
+    return (block, shared)
+
+
+def in_order(route, slots, place):
+    position = np.zeros((route.count,), np.int32)
+    for at, off in enumerate(route.offset):
+        position[off] = at
+    table = jnp.asarray(position)
+    owners = jnp.arange(route.count, dtype=jnp.int32)
+    return jnp.take(slots, table[owners ^ place], axis=0)
+
+
+def by_position(route, slots, place):
+    return jnp.take(slots, jnp.asarray(route.offset, jnp.int32) ^ place, axis=0)
+
+
+def wide_to_rows(shard, width):
+    rows = shard.shape[0]
+    return jnp.concatenate(
+        [shard[:, at * width : (at + 1) * width] for at in range(shard.shape[1] // width)]
+    )
+
+
+def rows_to_wide(slots, pieces):
+    owners, rows, width = slots.shape
+    each = rows // pieces
     return (
-        lax.all_gather(inner_part[0], "dp", axis=0, tiled=True),
-        lax.all_gather(inner_part[1], "dp", axis=0, tiled=True),
-        lax.all_gather(inner_part[2], "dp", axis=0, tiled=True),
-        lax.all_gather(inner_part[3], "dp", axis=0, tiled=True),
-        lax.all_gather(inner_part[4], "dp", axis=1, tiled=True),
-        lax.all_gather(inner_part[5], "dp", axis=1, tiled=True),
-    )
-
-
-def settle(local_grads):
-    outer_part = (
-        lax.psum_scatter(
-            local_grads[0].astype(jnp.bfloat16), "dp", scatter_dimension=0, tiled=True
-        ).astype(jnp.float32),
-        lax.psum_scatter(
-            local_grads[1].astype(jnp.bfloat16), "dp", scatter_dimension=0, tiled=True
-        ).astype(jnp.float32),
-        lax.psum_scatter(
-            local_grads[2].astype(jnp.bfloat16), "dp", scatter_dimension=0, tiled=True
-        ).astype(jnp.float32),
-        lax.psum_scatter(
-            local_grads[3].astype(jnp.bfloat16), "dp", scatter_dimension=0, tiled=True
-        ).astype(jnp.float32),
-        lax.psum_scatter(
-            local_grads[4].astype(jnp.bfloat16), "dp", scatter_dimension=1, tiled=True
-        ).astype(jnp.float32),
-        lax.psum_scatter(
-            local_grads[5].astype(jnp.bfloat16), "dp", scatter_dimension=1, tiled=True
-        ).astype(jnp.float32),
-    )
+        slots.reshape(owners, pieces, each, width)
+        .transpose(0, 2, 1, 3)
+        .reshape(owners * each, pieces * width)
+    )
+
+
+def wide_to_slots(grad, owners, width):
+    rows, total = grad.shape
+    pieces = total // width
     return (
-        lax.psum_scatter(
-            outer_part[0].astype(jnp.bfloat16), "fsdp", scatter_dimension=0, tiled=True
-        ).astype(jnp.float32),
-        lax.psum_scatter(
-            outer_part[1].astype(jnp.bfloat16), "fsdp", scatter_dimension=0, tiled=True
-        ).astype(jnp.float32),
-        lax.psum_scatter(
-            outer_part[2].astype(jnp.bfloat16), "fsdp", scatter_dimension=0, tiled=True
-        ).astype(jnp.float32),
-        lax.psum_scatter(
-            outer_part[3].astype(jnp.bfloat16), "fsdp", scatter_dimension=0, tiled=True
-        ).astype(jnp.float32),
-        lax.psum_scatter(
-            outer_part[4].astype(jnp.bfloat16), "fsdp", scatter_dimension=1, tiled=True
-        ).astype(jnp.float32),
-        lax.psum_scatter(
-            outer_part[5].astype(jnp.bfloat16), "fsdp", scatter_dimension=1, tiled=True
-        ).astype(jnp.float32),
-    )
-
+        grad.reshape(owners, rows // owners, pieces, width)
+        .transpose(0, 2, 1, 3)
+        .reshape(owners, pieces * (rows // owners), width)
+    )
 
 def advance(master, moment, average, grad, momentum, step_rate, decay_now):
     new_moment = momentum * moment + grad
@@ -333,8 +364,48 @@
         bias_average,
     )
     layers = attend_weight.shape[0]
+    model_width = attend_weight.shape[2] // 3
+    each = attend_weight.shape[1]
+    outer_size = lax.axis_size("dp")
+    inner_size = lax.axis_size("fsdp")
+    everyone = outer_size * inner_size
+    place = lax.axis_index("dp") * inner_size + lax.axis_index("fsdp")
+    first_route, second_route = routes(outer_size, inner_size)
+    low = lambda item: item.astype(jnp.bfloat16)
     onehot = (dataset_ids[:, None] == jnp.arange(NDS, dtype=jnp.int32)[None, :]).astype(jnp.float32)
-    counts = lax.psum(jnp.sum(onehot, axis=0), ("dp", "fsdp"))
+    mine = jnp.zeros((24, model_width), jnp.bfloat16)
+    vectors = jnp.concatenate(
+        [low(item[at]) for at in range(layers) for item in (norm_gains, bias_rows)]
+    )
+    mine = lax.dynamic_update_slice(mine, vectors, (0, place * vectors.shape[1]))
+    mine = mine.at[20, :NDS].set(low(jnp.sum(onehot, axis=0)))
+    gathered = []
+    for at in range(layers):
+        first = wide_to_rows(low(attend_weight[at]), model_width)
+        second = jnp.concatenate(
+            [
+                low(output_weight[at]),
+                wide_to_rows(low(expand_weight[at]), model_width),
+                low(shrink_weight[at]),
+            ]
+        )
+        first_all, mine_all = spread(first_route, first, mine if at == 0 else None)
+        second_all, _ = spread(second_route, second)
+        if at == 0:
+            vectors_all = mine_all
+        first_all = in_order(first_route, first_all, place)
+        second_all = in_order(second_route, second_all, place)
+        gathered.append(
+            (
+                rows_to_wide(first_all, 3),
+                second_all[:, :each].reshape(model_width, model_width),
+                rows_to_wide(second_all[:, each : 3 * each], 2),
+                second_all[:, 3 * each :].reshape(2 * model_width, model_width),
+                vectors_all[10 * at : 10 * at + 2],
+                vectors_all[10 * at + 2 : 10 * at + 10],
+            )
+        )
+    counts = vectors_all[20, :NDS].astype(jnp.float32)
     own_count = jnp.sum(onehot * counts[None, :], axis=1)
     row_weight = jnp.sum(counts) / (NDS * own_count)
     positions = jnp.arange(tokens.shape[1], dtype=jnp.int32)
@@ -344,19 +415,40 @@
     effective = cotangent.astype(jnp.float32) * (live_rows * row_weight[:, None])[:, :, None]
     current = tokens
     inputs_kept = []
-    gathered_kept = []
     for layer_index in range(layers):
-        weights = collect(masters, layer_index)
-        gathered_kept.append(weights)
         inputs_kept.append(current)
-        result, unused_kept = layer_forward(current, weights)
+        result, unused_kept = layer_forward(current, gathered[layer_index])
         current = result.astype(jnp.bfloat16)
     grad_rows = effective
     shard_grads = [None] * layers
     for layer_index in reversed(range(layers)):
-        weights = collect(masters, layer_index)
-        local_grads, grad_rows = layer_backward(inputs_kept[layer_index], weights, grad_rows)
-        shard_grads[layer_index] = settle(local_grads)
+        local, grad_rows = layer_backward(inputs_kept[layer_index], gathered[layer_index], grad_rows)
+        first = by_position(first_route, wide_to_slots(low(local[0]), everyone, model_width), place)
+        second = by_position(
+            second_route,
+            jnp.concatenate(
+                [
+                    low(local[1]).reshape(everyone, each, model_width),
+                    wide_to_slots(low(local[2]), everyone, model_width),
+                    low(local[3]).reshape(everyone, 2 * each, model_width),
+                ],
+                axis=1,
+            ),
+            place,
+        )
+        second_sum, _ = gather_sum(second_route, second)
+        shared = jnp.pad(low(jnp.concatenate([local[4], local[5]])), ((0, 6), (0, 0)))
+        first_sum, shared_sum = gather_sum(first_route, first, shared)
+        wide = lambda rows, pieces: rows_to_wide(rows[None], pieces).astype(jnp.float32)
+        own = lax.dynamic_slice(shared_sum, (0, place * each), (10, each)).astype(jnp.float32)
+        shard_grads[layer_index] = (
+            wide(first_sum, 3),
+            second_sum[:each].astype(jnp.float32),
+            wide(second_sum[each : 3 * each], 2),
+            second_sum[3 * each :].astype(jnp.float32),
+            own[:2],
+            own[2:],
+        )
     step_value = step_count[0].astype(jnp.float32)
     decay_now = average_decay[0] * (1.0 + step_value) / (4.0 + step_value)
     outputs = [current, grad_rows]

time: 1720 us -> 485 us (0.28)
  waiting for transfers between devices: 969 us -> 55.3 us
  blocking collectives: 458 us -> 0 us
  local copies, waits for them, and re-layouts: 55.4 us -> 148 us
  starting transfers between devices: 1.42 us -> 44.2 us
  other arithmetic: 56.7 us -> 94.5 us
  matrix products: 157 us -> 129 us
    reduce_scatter x12 -> x0, waiting for transfers between devices: 522 us -> none  [the longest x2 130 us: settle(): lax.psum_scatter(outer_part[2].astype(jnp.bfloat16), 'fsdp', scatter_dime...]
    unnamed x42 -> x0, waiting for transfers between devices: 447 us -> none
    all_gather x18 -> x0, blocking collectives: 419 us -> none  [the longest x2 67.8 us: collect(): lax.all_gather(pieces[0], 'fsdp', axis=0, tiled=True)]
    ppermute x0 -> x40, waiting for transfers between devices: none -> 55.3 us  [swap(): lax.ppermute(payload, axis, [(one, one ^ bit) for one in range(size)])]
    ppermute x0 -> x40, starting transfers between devices: none -> 44.2 us  [swap(): lax.ppermute(payload, axis, [(one, one ^ bit) for one in range(size)])]
    psum x1 -> x0, blocking collectives: 39.7 us -> none  [shards(): counts = lax.psum(jnp.sum(onehot, axis=0), ('dp', 'fsdp'))]
    gather x0 -> x10, local copies, waits for them, and re-layouts: none -> 26.9 us  [the longest x4 15 us: by_position(): return jnp.take(slots, jnp.asarray(route.offset, jnp.int32) ^ place, axis=0)]
    reshape x0 -> x6, local copies, waits for them, and re-layouts: none -> 20.4 us  [wide_to_slots(): grad.reshape(owners, rows // owners, pieces, width).transpose(0, 2, 1, 3)]
  transfers between devices with their start and end apart: 30 -> 40, of which waited for: 23 -> 16; matrix products, arithmetic and copies ran while one was open for 10% -> 31% of each run, Pallas kernels for 0% -> 0%
where the time goes in v1:
time: 485 us; the launch traced here: 479 us
  local copies, waits for them, and re-layouts  148 us (31%)
  matrix products  129 us (27%)
  other arithmetic  94.5 us (19%)
  waiting for transfers between devices  55.3 us (11%)
  starting transfers between devices  44.2 us (9%)
  between operations  8.34 us (2%)
    ppermute x40, waiting for transfers between devices, swap(): lax.ppermute(payload, axis, [(one, one ^ bit) for one in range(size)])  55.3 us
    unnamed x292, local copies, waits for them, and re-layouts  47.9 us
    ppermute x40, starting transfers between devices, swap(): lax.ppermute(payload, axis, [(one, one ^ bit) for one in range(size)])  44.2 us
    dot_general x2, matrix products, layer_forward(): jnp.dot(first_low, expand_w, preferred_element_type=jnp.float32)  22.2 us
    reshape x6, local copies, waits for them, and re-layouts, wide_to_slots(): grad.reshape(owners, rows // owners, pieces, width).transpose(0, 2, 1, 3)  20.4 us
    dot_general x2, matrix products, attend_one(): jnp.einsum('hqk,khe->qhe', softmax_low, value_rows, preferred_element_typ...  17.2 us
    convert_element_type x2, other arithmetic, attend_back(): grad_scores = (factor * softmax_rows * (grad_probs - jnp.sum(softmax_rows...  15.3 us
    reduce_sum x2, other arithmetic, attend_one(): jnp.sum(jnp.exp(scaled - row_top), axis=-1, keepdims=True)  15.2 us
  transfers between devices with their start and end apart: 40, of which 16 were waited for; matrix products, arithmetic and copies ran while one was open for 31% of the time, Pallas kernels for 0%

profile of v1, /device:TPU:0, one launch (start us, length us, event | category | flops | bytes accessed | tf_op | source)
XLA Modules:
  0.0 479.0 jit_solution(8876318222858137481)
XLA Ops:
  4.7 4.1 collective-permute-start.10
  55.8 4.6 collective-permute-done.17
  62.8 5.6 %collective-permute-done.13 = bf16[384,512]{1,0:T(8,128)(2,1)S(1)} collective-permute-done((bf16[384,512]{1,0:T(8,128)(2,1)}, bf16[384,512]{1,0:T(8,128)(2,1)S(1)}, u32[]{:S(2)}, u32[]{:S(2)}) %collective-permute-start.13) | collective-permute-done | bytes 393248 | tf_op jit(solution)/shard_map/ppermute | solution.py:235
  104.9 7.2 %multiply_reduce_fusion.3 = (f32[4,1024]{1,0:T(4,128)S(1)}, f32[4,1024,896]{1,2,0:T(8,128)}) fusion(bf16[1024,4,128]{0,2,1:T(8,128)(2,1)S(1)} %bitcast.369, bf16[896,4,128]{0,2,1:T(8,128)(2,1)S(1)} %bitcast.373), kind=kOutput, calls=%fused_computation.19 | convolution fusion | flops 946860032 | bytes 16662528 | tf_op jit(solution)/shard_map/while/body/eval_jaxpr/qhe,khe->hqk/dot_general | solution.py:44
  112.1 7.6 %exponential_reduce_fusion.1 = f32[4,1024]{1,0:T(4,128)S(1)} fusion(f32[4,1024,896]{1,2,0:T(8,128)} %get-tuple-element.479, f32[4,1024]{1,0:T(4,128)S(1)} %get-tuple-element.478), kind=kLoop, calls=%fused_computation.17 | loop fusion | flops 11005952 | bytes 14712832 | tf_op jit(solution)/shard_map/while/body/eval_jaxpr/reduce_sum | solution.py:47
  126.2 9.2 %convolution_convert_fusion.9 = bf16[4,128,1024]{2,1,0:T(8,128)(2,1)} fusion(bf16[896,4,128]{0,2,1:T(8,128)(2,1)S(1)} %bitcast.387, f32[4,1024,896]{1,2,0:T(8,128)} %get-tuple-element.479, f32[4,1024]{1,0:T(4,128)S(1)} %log_add_fusion.1), kind=kOutput, calls=%fused_computation.155 | convolution fusion | flops 951058432 | bytes 16662528 | tf_op jit(solution)/shard_map/while/body/eval_jaxpr/hqk,khe->qhe/dot_general | solution.py:49
  153.8 11.8 %fusion.4 = (bf16[1024,1024]{1,0:T(8,128)(2,1)S(1)}, f32[1024,1024]{1,0:T(8,128)}) fusion(f32[1024]{0:T(1024)S(1)} %bitcast.467, bf16[512,1024]{1,0:T(8,128)(2,1)S(1)} %bitcast.429, f32[1,1024,512]{1,2,0:T(8,128)S(1)} %get-tuple-element.481, f32[512]{0:T(512)S(1)} %bitcast.471, f32[512]{0:T(512)S(1)} %bitcast.451, f32[1024]{0:T(1024)S(1)} %add_rsqrt_fusion.3, ...), kind=kOutput, calls=%fused_computation.30 | convolution fusion | flops 1145569280 | bytes 9453568 | tf_op jit(solution)/shard_map/dot_general | solution.py:113
  178.7 7.3 %multiply_reduce_fusion.2 = (f32[4,1024]{1,0:T(4,128)S(1)}, f32[4,1024,896]{1,2,0:T(8,128)}) fusion(bf16[1024,4,128]{0,2,1:T(8,128)(2,1)S(1)} %bitcast.371, bf16[896,4,128]{0,2,1:T(8,128)(2,1)S(1)} %bitcast.375), kind=kOutput, calls=%fused_computation.18 | convolution fusion | flops 946860032 | bytes 16662528 | tf_op jit(solution)/shard_map/while/body/eval_jaxpr/qhe,khe->hqk/dot_general | solution.py:44
  186.0 7.6 %exponential_reduce_fusion = f32[4,1024]{1,0:T(4,128)S(1)} fusion(f32[4,1024,896]{1,2,0:T(8,128)} %get-tuple-element.487, f32[4,1024]{1,0:T(4,128)S(1)} %get-tuple-element.486), kind=kLoop, calls=%fused_computation.15 | loop fusion | flops 11005952 | bytes 14712832 | tf_op jit(solution)/shard_map/while/body/eval_jaxpr/reduce_sum | solution.py:47
  193.6 8.0 %convolution_convert_fusion.8 = bf16[4,128,1024]{2,1,0:T(8,128)(2,1)S(1)} fusion(f32[4,1024,896]{1,2,0:T(8,128)} %get-tuple-element.487, f32[4,1024]{1,0:T(4,128)S(1)} %log_add_fusion, bf16[896,4,128]{2,1,0:T(4,128)(2,1)S(1)} %squeeze.117), kind=kOutput, calls=%fused_computation.154 | convolution fusion | flops 951058432 | bytes 16662528 | tf_op jit(solution)/shard_map/while/body/eval_jaxpr/hqk,khe->qhe/dot_general | solution.py:49
  202.9 10.4 %fusion.7 = (bf16[1024,1024]{1,0:T(8,128)(2,1)S(1)}, f32[1024,1024]{1,0:T(8,128)S(1)}) fusion(f32[1024]{0:T(1024)S(1)} %bitcast.469, bf16[512,1024]{1,0:T(8,128)(2,1)S(1)} %bitcast.431, f32[1,1024,512]{1,2,0:T(8,128)S(1)} %get-tuple-element.489, f32[512]{0:T(512)S(1)} %bitcast.474, f32[512]{0:T(512)S(1)} %bitcast.456, f32[1024]{0:T(1024)S(1)} %add_rsqrt_fusion.1, ...), kind=kOutput, calls=%fused_computation.33 | convolution fusion | flops 1145569280 | bytes 9453568 | tf_op jit(solution)/shard_map/dot_general | solution.py:113
  240.5 6.9 %multiply_reduce_fusion.1 = (f32[4,1024]{1,0:T(4,128)S(1)}, f32[4,1024,896]{1,2,0:T(8,128)}) fusion(f32[4,1024,896]{1,2,0:T(8,128)S(1)} %bitcast.364, f32[4,1024]{1,0:T(4,128)S(1)} %log_add_fusion, bf16[1024,4,128]{0,2,1:T(8,128)(2,1)S(1)} %bitcast.368, bf16[896,4,128]{2,1,0:T(4,128)(2,1)S(1)} %squeeze.117), kind=kOutput, calls=%fused_computation.13 | convolution fusion | flops 954200064 | bytes 31358976 | tf_op jit(solution)/shard_map/while/body/eval_jaxpr/qhe,khe->hqk/dot_general | solution.py:66
  247.4 7.8 %multiply_convert_fusion.1 = bf16[4,1024,896]{1,2,0:T(8,128)(2,1)S(1)} fusion(f32[4,1024,896]{1,2,0:T(8,128)} %get-tuple-element.496, f32[4,1024,896]{1,2,0:T(8,128)S(1)} %bitcast.364, f32[4,1024]{1,0:T(4,128)S(1)} %get-tuple-element.495, f32[4,1024]{1,0:T(4,128)S(1)} %log_add_fusion), kind=kLoop, calls=%fused_computation.12 | loop fusion | flops 22020096 | bytes 36732928 | tf_op jit(solution)/shard_map/while/body/eval_jaxpr/convert_element_type | solution.py:73
  288.3 7.0 %multiply_reduce_fusion = (f32[4,1024]{1,0:T(4,128)S(1)}, f32[4,1024,896]{1,2,0:T(8,128)}) fusion(f32[4,1024,896]{1,2,0:T(8,128)S(1)} %bitcast.366, f32[4,1024]{1,0:T(4,128)S(1)} %copy-done.68, bf16[1024,4,128]{0,2,1:T(8,128)(2,1)S(1)} %bitcast.378, bf16[896,4,128]{0,2,1:T(8,128)(2,1)S(1)} %bitcast.388), kind=kOutput, calls=%fused_computation.11 | convolution fusion | flops 954200064 | bytes 31358976 | tf_op jit(solution)/shard_map/while/body/eval_jaxpr/qhe,khe->hqk/dot_general | solution.py:66
  295.2 7.5 %multiply_convert_fusion = bf16[4,1024,896]{1,2,0:T(8,128)(2,1)S(1)} fusion(f32[4,1024,896]{1,2,0:T(8,128)} %get-tuple-element.500, f32[4,1024,896]{1,2,0:T(8,128)S(1)} %bitcast.366, f32[4,1024]{1,0:T(4,128)S(1)} %get-tuple-element.499, f32[4,1024]{1,0:T(4,128)S(1)} %copy-done.68), kind=kLoop, calls=%fused_computation.10 | loop fusion | flops 22020096 | bytes 36732928 | tf_op jit(solution)/shard_map/while/body/eval_jaxpr/convert_element_type | solution.py:73
  323.7 4.1 gather_fusion.9
  330.9 4.1 gather_fusion.8
  335.0 4.6 broadcast_select_fusion.1
  342.6 5.6 %reshape.1055 = bf16[32,16,3,512]{3,2,1,0:T(4,128)(2,1)} reshape(bf16[512,1536]{1,0:T(8,128)(2,1)} %convolution_convert_fusion) | data formatting | bytes 3145728 | tf_op jit(solution)/shard_map/reshape | solution.py:309
  351.9 4.2 fusion.36
  360.9 5.6 %reshape.1052 = bf16[32,16,3,512]{3,2,1,0:T(4,128)(2,1)} reshape(bf16[512,1536]{1,0:T(8,128)(2,1)} %copy.162) | data formatting | bytes 3145728 | tf_op jit(solution)/shard_map/reshape | solution.py:309
  398.0 8.1 %collective-permute-done.21 = bf16[400,512]{1,0:T(8,128)(2,1)S(1)} collective-permute-done((bf16[400,512]{1,0:T(8,128)(2,1)S(1)}, bf16[400,512]{1,0:T(8,128)(2,1)S(1)}, u32[]{:S(2)}, u32[]{:S(2)}) %collective-permute-start.21) | collective-permute-done | bytes 409632 | tf_op jit(solution)/shard_map/ppermute | solution.py:235
  407.9 6.4 %collective-permute-done.26 = bf16[400,512]{1,0:T(8,128)(2,1)S(1)} collective-permute-done((bf16[400,512]{1,0:T(8,128)(2,1)S(1)}, bf16[400,512]{1,0:T(8,128)(2,1)S(1)}, u32[]{:S(2)}, u32[]{:S(2)}) %collective-permute-start.26) | collective-permute-done | bytes 409632 | tf_op jit(solution)/shard_map/ppermute | solution.py:235
  452.8 5.4 %collective-permute-done.32 = bf16[320,512]{1,0:T(8,128)(2,1)S(1)} collective-permute-done((bf16[320,512]{1,0:T(8,128)(2,1)S(1)}, bf16[320,512]{1,0:T(8,128)(2,1)S(1)}, u32[]{:S(2)}, u32[]{:S(2)}) %collective-permute-start.32) | collective-permute-done | bytes 327712 | tf_op jit(solution)/shard_map/ppermute | solution.py:235
  (635 shorter events, 310.0 us)
Async XLA Ops:
  4.7 23.7 %collective-permute-start.10 = (bf16[48,512]{1,0:T(8,128)(2,1)S(1)}, bf16[48,512]{1,0:T(8,128)(2,1)S(1)}, u32[]{:S(2)}, u32[]{:S(2)}) collective-permute-start(bf16[48,512]{1,0:T(8,128)(2,1)S(1)} %pad_maximum_fusion.25), channel_id=1, source_target_pairs={{0,4},{1,5},{2,6},{3,7},{4,0},{5,1},{6,2},{7,3},{8,12},{9,13},{10,... | collective-permute-start | bytes 147464 | tf_op jit(solution)/shard_map/ppermute | solution.py:235
  11.6 19.5 %collective-permute-start = (bf16[72,512]{1,0:T(8,128)(2,1)S(1)}, bf16[72,512]{1,0:T(8,128)(2,1)S(1)}, u32[]{:S(2)}, u32[]{:S(2)}) collective-permute-start(bf16[72,512]{1,0:T(8,128)(2,1)S(1)} %pad_maximum_fusion.20), channel_id=1, source_target_pairs={{0,4},{1,5},{2,6},{3,7},{4,0},{5,1},{6,2},{7,3},{8,12},{9,13},{10,... | collective-permute-start | bytes 221192 | tf_op jit(solution)/shard_map/ppermute | solution.py:235
  16.6 16.0 %collective-permute-start.5 = (bf16[80,512]{1,0:T(8,128)(2,1)S(1)}, bf16[80,512]{1,0:T(8,128)(2,1)S(1)}, u32[]{:S(2)}, u32[]{:S(2)}) collective-permute-start(bf16[80,512]{1,0:T(8,128)(2,1)S(1)} %pad_maximum_fusion.18), channel_id=1, source_target_pairs={{0,4},{1,5},{2,6},{3,7},{4,0},{5,1},{6,2},{7,3},{8,12},{9,13},{10,... | collective-permute-start | bytes 245768 | tf_op jit(solution)/shard_map/ppermute | solution.py:235
  19.9 15.4 %collective-permute-start.15 = (bf16[80,512]{1,0:T(8,128)(2,1)S(1)}, bf16[80,512]{1,0:T(8,128)(2,1)S(1)}, u32[]{:S(2)}, u32[]{:S(2)}) collective-permute-start(bf16[80,512]{1,0:T(8,128)(2,1)S(1)} %pad_maximum_fusion.19), channel_id=1, source_target_pairs={{0,4},{1,5},{2,6},{3,7},{4,0},{5,1},{6,2},{7,3},{8,12},{9,13},{10,... | collective-permute-start | bytes 245768 | tf_op jit(solution)/shard_map/ppermute | solution.py:235
  42.6 10.8 %collective-permute-start.7 = (bf16[320,512]{1,0:T(8,128)(2,1)}, bf16[320,512]{1,0:T(8,128)(2,1)S(1)}, u32[]{:S(2)}, u32[]{:S(2)}) collective-permute-start(bf16[320,512]{1,0:T(8,128)(2,1)} %get-tuple-element.328), channel_id=1, source_target_pairs={{0,16},{8,24},{16,0},{24,8},{1,17},{9,25},{17,1},{25,9},{2,18},{10... | collective-permute-start | bytes 983048 | tf_op jit(solution)/shard_map/ppermute | solution.py:235
  45.0 15.5 %collective-permute-start.17 = (bf16[320,512]{1,0:T(8,128)(2,1)}, bf16[320,512]{1,0:T(8,128)(2,1)S(1)}, u32[]{:S(2)}, u32[]{:S(2)}) collective-permute-start(bf16[320,512]{1,0:T(8,128)(2,1)} %get-tuple-element.332), channel_id=1, source_target_pairs={{0,16},{8,24},{16,0},{24,8},{1,17},{9,25},{17,1},{25,9},{2,18},{10... | collective-permute-start | bytes 983048 | tf_op jit(solution)/shard_map/ppermute | solution.py:235
  46.6 21.7 %collective-permute-start.13 = (bf16[384,512]{1,0:T(8,128)(2,1)}, bf16[384,512]{1,0:T(8,128)(2,1)S(1)}, u32[]{:S(2)}, u32[]{:S(2)}) collective-permute-start(bf16[384,512]{1,0:T(8,128)(2,1)} %get-tuple-element.324), channel_id=1, source_target_pairs={{0,16},{8,24},{16,0},{24,8},{1,17},{9,25},{17,1},{25,9},{2,18},{10... | collective-permute-start | bytes 1179656 | tf_op jit(solution)/shard_map/ppermute | solution.py:235
  49.5 23.3 %collective-permute-start.3 = (bf16[408,512]{1,0:T(8,128)(2,1)}, bf16[408,512]{1,0:T(8,128)(2,1)S(1)}, u32[]{:S(2)}, u32[]{:S(2)}) collective-permute-start(bf16[408,512]{1,0:T(8,128)(2,1)} %constant_dynamic-update-slice_fusion.11), channel_id=1, source_target_pairs={{0,16},{8,24},{16,0},{24,8},{1,17},{9,25},{17,1},{25,9},{2,18},{10... | collective-permute-start | bytes 1253384 | tf_op jit(solution)/shard_map/ppermute | solution.py:235
  54.5 29.5 %collective-permute-start.8 = (bf16[640,512]{1,0:T(8,128)(2,1)}, bf16[640,512]{1,0:T(8,128)(2,1)}, u32[]{:S(2)}, u32[]{:S(2)}) collective-permute-start(bf16[640,512]{1,0:T(8,128)(2,1)} %get-tuple-element.315), channel_id=1, source_target_pairs={{0,1},{1,0},{2,3},{3,2},{4,5},{5,4},{6,7},{7,6},{8,9},{9,8},{10,11... | collective-permute-start | bytes 1966088 | tf_op jit(solution)/shard_map/ppermute | solution.py:235
  61.4 25.4 %collective-permute-start.18 = (bf16[640,512]{1,0:T(8,128)(2,1)}, bf16[640,512]{1,0:T(8,128)(2,1)}, u32[]{:S(2)}, u32[]{:S(2)}) collective-permute-start(bf16[640,512]{1,0:T(8,128)(2,1)} %get-tuple-element.318), channel_id=1, source_target_pairs={{0,1},{1,0},{2,3},{3,2},{4,5},{5,4},{6,7},{7,6},{8,9},{9,8},{10,11... | collective-permute-start | bytes 1966088 | tf_op jit(solution)/shard_map/ppermute | solution.py:235
  69.3 19.6 %collective-permute-start.14 = (bf16[768,512]{1,0:T(8,128)(2,1)}, bf16[768,512]{1,0:T(8,128)(2,1)}, u32[]{:S(2)}, u32[]{:S(2)}) collective-permute-start(bf16[768,512]{1,0:T(8,128)(2,1)} %get-tuple-element.311), channel_id=1, source_target_pairs={{0,8},{8,0},{16,24},{24,16},{1,9},{9,1},{17,25},{25,17},{2,10},{10... | collective-permute-start | bytes 2359304 | tf_op jit(solution)/shard_map/ppermute | solution.py:235
  74.5 19.2 %collective-permute-start.4 = (bf16[792,512]{1,0:T(8,128)(2,1)}, bf16[792,512]{1,0:T(8,128)(2,1)S(1)}, u32[]{:S(2)}, u32[]{:S(2)}) collective-permute-start(bf16[792,512]{1,0:T(8,128)(2,1)} %constant_dynamic-update-slice_fusion.18), channel_id=1, source_target_pairs={{0,8},{8,0},{16,24},{24,16},{1,9},{9,1},{17,25},{25,17},{2,10},{10... | collective-permute-start | bytes 2433032 | tf_op jit(solution)/shard_map/ppermute | solution.py:235
  86.3 49.1 %collective-permute-start.9 = (bf16[1280,512]{1,0:T(8,128)(2,1)}, bf16[1280,512]{1,0:T(8,128)(2,1)}, u32[]{:S(2)}, u32[]{:S(2)}) collective-permute-start(bf16[1280,512]{1,0:T(8,128)(2,1)} %get-tuple-element.305), channel_id=1, source_target_pairs={{0,8},{8,0},{16,24},{24,16},{1,9},{9,1},{17,25},{25,17},{2,10},{10... | collective-permute-start | bytes 3932168 | tf_op jit(solution)/shard_map/ppermute | solution.py:235
  88.9 51.9 %collective-permute-start.19 = (bf16[1280,512]{1,0:T(8,128)(2,1)}, bf16[1280,512]{1,0:T(8,128)(2,1)}, u32[]{:S(2)}, u32[]{:S(2)}) collective-permute-start(bf16[1280,512]{1,0:T(8,128)(2,1)} %get-tuple-element.307), channel_id=1, source_target_pairs={{0,8},{8,0},{16,24},{24,16},{1,9},{9,1},{17,25},{25,17},{2,10},{10... | collective-permute-start | bytes 3932168 | tf_op jit(solution)/shard_map/ppermute | solution.py:235
  351.6 64.4 %collective-permute-start.30 = (bf16[1280,512]{1,0:T(8,128)(2,1)}, bf16[1280,512]{1,0:T(8,128)(2,1)}, u32[]{:S(2)}, u32[]{:S(2)}) collective-permute-start(bf16[1280,512]{1,0:T(8,128)(2,1)} %bitcast.116), channel_id=1, source_target_pairs={{0,8},{8,0},{16,24},{24,16},{1,9},{9,1},{17,25},{25,17},{2,10},{10... | collective-permute-start | bytes 3932168 | tf_op jit(solution)/shard_map/ppermute | solution.py:235
  380.7 10.6 %collective-permute-start.20 = (bf16[784,512]{1,0:T(8,128)(2,1)}, bf16[784,512]{1,0:T(8,128)(2,1)}, u32[]{:S(2)}, u32[]{:S(2)}) collective-permute-start(bf16[784,512]{1,0:T(8,128)(2,1)} %pad_maximum_fusion.8), channel_id=1, source_target_pairs={{0,8},{8,0},{16,24},{24,16},{1,9},{9,1},{17,25},{25,17},{2,10},{10... | collective-permute-start | bytes 2408456 | tf_op jit(solution)/shard_map/ppermute | solution.py:235
  382.8 12.5 %collective-permute-start.25 = (bf16[784,512]{1,0:T(8,128)(2,1)}, bf16[784,512]{1,0:T(8,128)(2,1)}, u32[]{:S(2)}, u32[]{:S(2)}) collective-permute-start(bf16[784,512]{1,0:T(8,128)(2,1)} %pad_maximum_fusion.9), channel_id=1, source_target_pairs={{0,8},{8,0},{16,24},{24,16},{1,9},{9,1},{17,25},{25,17},{2,10},{10... | collective-permute-start | bytes 2408456 | tf_op jit(solution)/shard_map/ppermute | solution.py:235
  388.0 30.4 %collective-permute-start.35 = (bf16[1280,512]{1,0:T(8,128)(2,1)}, bf16[1280,512]{1,0:T(8,128)(2,1)}, u32[]{:S(2)}, u32[]{:S(2)}) collective-permute-start(bf16[1280,512]{1,0:T(8,128)(2,1)} %bitcast.124), channel_id=1, source_target_pairs={{0,8},{8,0},{16,24},{24,16},{1,9},{9,1},{17,25},{25,17},{2,10},{10... | collective-permute-start | bytes 3932168 | tf_op jit(solution)/shard_map/ppermute | solution.py:235
  393.7 12.4 %collective-permute-start.21 = (bf16[400,512]{1,0:T(8,128)(2,1)S(1)}, bf16[400,512]{1,0:T(8,128)(2,1)S(1)}, u32[]{:S(2)}, u32[]{:S(2)}) collective-permute-start(bf16[400,512]{1,0:T(8,128)(2,1)S(1)} %pad_maximum_fusion.10), channel_id=1, source_target_pairs={{0,16},{8,24},{16,0},{24,8},{1,17},{9,25},{17,1},{25,9},{2,18},{10... | collective-permute-start | bytes 1228808 | tf_op jit(solution)/shard_map/ppermute | solution.py:235
  397.5 16.8 %collective-permute-start.26 = (bf16[400,512]{1,0:T(8,128)(2,1)S(1)}, bf16[400,512]{1,0:T(8,128)(2,1)S(1)}, u32[]{:S(2)}, u32[]{:S(2)}) collective-permute-start(bf16[400,512]{1,0:T(8,128)(2,1)S(1)} %pad_maximum_fusion.11), channel_id=1, source_target_pairs={{0,16},{8,24},{16,0},{24,8},{1,17},{9,25},{17,1},{25,9},{2,18},{10... | collective-permute-start | bytes 1228808 | tf_op jit(solution)/shard_map/ppermute | solution.py:235
  406.3 16.2 %collective-permute-start.22 = (bf16[208,512]{1,0:T(8,128)(2,1)S(1)}, bf16[208,512]{1,0:T(8,128)(2,1)S(1)}, u32[]{:S(2)}, u32[]{:S(2)}) collective-permute-start(bf16[208,512]{1,0:T(8,128)(2,1)S(1)} %pad_maximum_fusion.12), channel_id=1, source_target_pairs={{0,1},{1,0},{2,3},{3,2},{4,5},{5,4},{6,7},{7,6},{8,9},{9,8},{10,11... | collective-permute-start | bytes 638984 | tf_op jit(solution)/shard_map/ppermute | solution.py:235
  417.8 28.9 %collective-permute-start.31 = (bf16[640,512]{1,0:T(8,128)(2,1)S(1)}, bf16[640,512]{1,0:T(8,128)(2,1)}, u32[]{:S(2)}, u32[]{:S(2)}) collective-permute-start(bf16[640,512]{1,0:T(8,128)(2,1)S(1)} %slice.775), channel_id=1, source_target_pairs={{0,1},{1,0},{2,3},{3,2},{4,5},{5,4},{6,7},{7,6},{8,9},{9,8},{10,11... | collective-permute-start | bytes 1966088 | tf_op jit(solution)/shard_map/ppermute | solution.py:235
  421.0 28.6 %collective-permute-start.36 = (bf16[640,512]{1,0:T(8,128)(2,1)}, bf16[640,512]{1,0:T(8,128)(2,1)}, u32[]{:S(2)}, u32[]{:S(2)}) collective-permute-start(bf16[640,512]{1,0:T(8,128)(2,1)} %slice.786), channel_id=1, source_target_pairs={{0,1},{1,0},{2,3},{3,2},{4,5},{5,4},{6,7},{7,6},{8,9},{9,8},{10,11... | collective-permute-start | bytes 1966088 | tf_op jit(solution)/shard_map/ppermute | solution.py:235
  450.9 11.2 %collective-permute-start.37 = (bf16[320,512]{1,0:T(8,128)(2,1)S(1)}, bf16[320,512]{1,0:T(8,128)(2,1)S(1)}, u32[]{:S(2)}, u32[]{:S(2)}) collective-permute-start(bf16[320,512]{1,0:T(8,128)(2,1)S(1)} %slice.788), channel_id=1, source_target_pairs={{0,16},{8,24},{16,0},{24,8},{1,17},{9,25},{17,1},{25,9},{2,18},{10... | collective-permute-start | bytes 983048 | tf_op jit(solution)/shard_map/ppermute | solution.py:235
  (141 other events, 1005.6 us)

commit v2 on v1

v2 whole, which is shorter than its diff:
```python
import functools

import jax
import jax.numpy as jnp
import numpy as np
from jax import lax
from jax.experimental import pallas as pl
from jax.experimental.pallas import tpu as pltpu
from jax.sharding import PartitionSpec as P

HEADS = 4
CTX = 896
NDS = 8
EPS = 1e-05
OWNERS = 32
FIRST_PARTS = (16, 16, 16)
SECOND_PARTS = (16, 16, 16, 32)

SCORE_BLOCK = 256
ROW_BLOCK = 256
ROOT_HALF = 0.7071067811865476
PDF_PEAK = 0.3989422804014327
VMEM_LIMIT = 60 * 1024 * 1024
FLOAT = jnp.float32
HALF = jnp.bfloat16


def product(left, right, left_dim, right_dim):
    return lax.dot_general(
        left, right, (((left_dim,), (right_dim,)), ((), ())), preferred_element_type=FLOAT
    )


def owner_rows(offset, place, rows):
    return pl.ds(pl.multiple_of((offset ^ place) * rows, rows), rows)


def attend_kernel(offsets, place_ref, x_ref, near_ref, far_ref, vec_ref, joint_ref, probs_ref,
                  mixed_ref, weight_ref):
    head = pl.program_id(0)
    head_size = mixed_ref.shape[1]
    place = place_ref[0]

    half = len(offsets) // 2
    for at, offset in enumerate(offsets):
        slots = near_ref if at < half else far_ref
        rows = owner_rows(offset, place, 16)
        for piece in range(3):
            weight_ref[0, rows, piece * head_size : (piece + 1) * head_size] = slots[
                at % half, piece * 16 : (piece + 1) * 16, :
            ]
    zeros = jnp.zeros((1, head_size), FLOAT)
    shift = jnp.concatenate([vec_ref[2:3, :], zeros, vec_ref[3:4, :]], axis=1)
    joint_ref[0] = (product(x_ref[...], weight_ref[0], 1, 0) + shift).astype(HALF)
    keys = joint_ref[0, :CTX, head_size : 2 * head_size]
    values = joint_ref[0, :CTX, 2 * head_size :]
    values_turned = jnp.transpose(values)
    factor = head_size ** (-0.5) * 1.4426950408889634
    for start in range(0, x_ref.shape[0], SCORE_BLOCK):
        span = slice(start, start + SCORE_BLOCK)
        queries = joint_ref[0, span, :head_size]
        scores = product(keys, queries, 1, 1)
        top = jnp.max(scores, axis=0, keepdims=True)
        grown = jnp.exp2((scores - top) * factor)
        total = jnp.sum(grown, axis=0, keepdims=True)
        probs = (grown * (1.0 / total)).astype(HALF)
        probs_ref[0, :, span] = probs
        mixed_ref[span, :] = jnp.transpose(product(values_turned, probs, 1, 0)).astype(HALF)


def attend_call(offsets, place, x, near, far, vectors):
    rows, width = x.shape
    head_size = width // HEADS
    slots, high, _ = near.shape
    return pl.pallas_call(
        functools.partial(attend_kernel, offsets),
        grid_spec=pltpu.PrefetchScalarGridSpec(
            num_scalar_prefetch=1,
            grid=(HEADS,),
            in_specs=[
                pl.BlockSpec((rows, width), lambda h, p: (0, 0)),
                pl.BlockSpec((slots, high, head_size), lambda h, p: (0, 0, h)),
                pl.BlockSpec((slots, high, head_size), lambda h, p: (0, 0, h)),
                pl.BlockSpec((16, head_size), lambda h, p: (0, h)),
            ],
            out_specs=[
                pl.BlockSpec((1, rows, 3 * head_size), lambda h, p: (h, 0, 0)),
                pl.BlockSpec((1, CTX, rows), lambda h, p: (h, 0, 0)),
                pl.BlockSpec((rows, head_size), lambda h, p: (0, h)),
                pl.BlockSpec((1, width, 3 * head_size), lambda h, p: (h, 0, 0)),
            ],
        ),
        out_shape=[
            jax.ShapeDtypeStruct((HEADS, rows, 3 * head_size), HALF),
            jax.ShapeDtypeStruct((HEADS, CTX, rows), HALF),
            jax.ShapeDtypeStruct((rows, width), HALF),
            jax.ShapeDtypeStruct((HEADS, width, 3 * head_size), HALF),
        ],
        compiler_params=pltpu.CompilerParams(vmem_limit_bytes=VMEM_LIMIT),
        cost_estimate=pl.CostEstimate(
            flops=2 * rows * width * 3 * width + 4 * rows * CTX * width,
            bytes_accessed=16 * 1024 * 1024,
            transcendentals=HEADS * rows * CTX,
        ),
        name="attend",
    )(place, x, near, far, vectors)


def unpack_second(offsets, place, near_ref, far_ref, output_w, expand_w, shrink_w):
    half = len(offsets) // 2
    width = output_w.shape[1]
    for at, offset in enumerate(offsets):
        slots = near_ref if at < half else far_ref
        rows = owner_rows(offset, place, 16)
        output_w[rows, :] = slots[at % half, 0:16, :]
        expand_w[rows, :width] = slots[at % half, 16:32, :]
        expand_w[rows, width:] = slots[at % half, 32:48, :]
        shrink_w[owner_rows(offset, place, 32), :] = slots[at % half, 48:80, :]


def row_mean(rows):
    return jnp.mean(rows, axis=-1, keepdims=True)


def normalize(rows):
    centred = rows - row_mean(rows)
    inv_std = lax.rsqrt(row_mean(centred * centred) + EPS)
    return (centred * inv_std, inv_std)


def forward_rows(x_ref, mixed_ref, vec_ref, output_w, expand_w, shrink_w):
    attn_out = product(mixed_ref[...], output_w[...], 1, 0) + vec_ref[4:5, :]
    unit_one, inv_one = normalize(x_ref[...].astype(FLOAT) + attn_out)
    first_norm = unit_one * vec_ref[0:1, :] + vec_ref[6:7, :]
    first_low = first_norm.astype(HALF)
    shift = jnp.concatenate([vec_ref[8:9, :], vec_ref[9:10, :]], axis=1)
    hidden = product(first_low, expand_w[...], 1, 0) + shift
    normal_cdf = 0.5 * (1.0 + lax.erf(hidden * ROOT_HALF))
    act_low = (hidden * normal_cdf).astype(HALF)
    slope = normal_cdf + hidden * (jnp.exp(-0.5 * hidden * hidden) * PDF_PEAK)
    branch = product(act_low, shrink_w[...], 1, 0) + vec_ref[5:6, :]
    unit_two, inv_two = normalize(first_norm + branch)
    result = unit_two * vec_ref[1:2, :] + vec_ref[7:8, :]
    return (unit_one, inv_one, first_low, act_low, slope, unit_two, inv_two, result)


def column_sum(rows):
    return jnp.sum(rows, axis=0, keepdims=True)


def backward_rows(grad_rows, mixed_ref, vec_ref, kept, output_w, expand_w, shrink_w, grad_mixed_ref,
                  grad_one_ref, grad_output, grad_expand, grad_shrink, sums):
    unit_one, inv_one, first_low, act_low, slope, unit_two, inv_two = kept
    width = grad_rows.shape[1]

    def layer_norm_back(rows, unit_rows, inv_std, gain):
        scaled = rows * gain
        return inv_std * (scaled - row_mean(scaled) - unit_rows * row_mean(scaled * unit_rows))

    grad_two = layer_norm_back(grad_rows, unit_two, inv_two, vec_ref[1:2, :])
    branch_low = grad_two.astype(HALF)
    grad_shrink[...] += product(act_low, branch_low, 0, 0)
    grad_hidden = (product(branch_low, shrink_w[...], 1, 1) * slope).astype(HALF)
    grad_expand[...] += product(first_low, grad_hidden, 0, 0)
    grad_first = grad_two + product(grad_hidden, expand_w[...], 1, 1)
    grad_one = layer_norm_back(grad_first, unit_one, inv_one, vec_ref[0:1, :])
    attn_low = grad_one.astype(HALF)
    grad_output[...] += product(mixed_ref[...], attn_low, 0, 0)
    grad_mixed_ref[...] = product(attn_low, output_w[...], 1, 1).astype(HALF)
    grad_one_ref[...] = grad_one
    sums[0:1, :] += column_sum(grad_first * unit_one)
    sums[1:2, :] += column_sum(grad_rows * unit_two)
    sums[4:5, :] += column_sum(attn_low.astype(FLOAT))
    sums[5:6, :] += column_sum(branch_low.astype(FLOAT))
    sums[6:7, :] += column_sum(grad_first)
    sums[7:8, :] += column_sum(grad_rows)
    hidden_sum = column_sum(grad_hidden.astype(FLOAT))
    sums[8:9, :] += hidden_sum[:, :width]
    sums[9:10, :] += hidden_sum[:, width:]


def pack_second(offsets, place, slots_ref, grad_output, grad_expand, grad_shrink):
    width = grad_output.shape[1]
    for at, offset in enumerate(offsets):
        rows = owner_rows(offset, place, 16)
        slots_ref[at, 0:16, :] = grad_output[rows, :].astype(HALF)
        slots_ref[at, 16:32, :] = grad_expand[rows, :width].astype(HALF)
        slots_ref[at, 32:48, :] = grad_expand[rows, width:].astype(HALF)
        slots_ref[at, 48:80, :] = grad_shrink[owner_rows(offset, place, 32), :].astype(HALF)


def dense_kernel(offsets, place_ref, x_ref, mixed_ref, near_ref, far_ref, vec_ref, result_ref,
                 unit_one_ref, inv_one_ref, act_ref, slope_ref, unit_two_ref, inv_two_ref,
                 output_w, expand_w, shrink_w):
    @pl.when(pl.program_id(0) == 0)
    def _():
        unpack_second(offsets, place_ref[0], near_ref, far_ref, output_w, expand_w, shrink_w)

    unit_one, inv_one, _, act_low, slope, unit_two, inv_two, result = forward_rows(
        x_ref, mixed_ref, vec_ref, output_w, expand_w, shrink_w
    )
    result_ref[...] = result.astype(HALF)
    unit_one_ref[...] = unit_one
    inv_one_ref[...] = inv_one
    act_ref[...] = act_low
    slope_ref[...] = slope
    unit_two_ref[...] = unit_two
    inv_two_ref[...] = inv_two


def dense_back_kernel(offsets, place_ref, grad_ref, mixed_ref, vec_ref, unit_one_ref, inv_one_ref,
                      act_ref, slope_ref, unit_two_ref, inv_two_ref, output_w, expand_w, shrink_w,
                      grad_mixed_ref, grad_one_ref, slots_ref, sums, grad_output, grad_expand,
                      grad_shrink):
    @pl.when(pl.program_id(0) == 0)
    def _():
        for item in (sums, grad_output, grad_expand, grad_shrink):
            item[...] = jnp.zeros_like(item)

    unit_one = unit_one_ref[...]
    first_low = (unit_one * vec_ref[0:1, :] + vec_ref[6:7, :]).astype(HALF)
    kept = (unit_one, inv_one_ref[...], first_low, act_ref[...], slope_ref[...], unit_two_ref[...],
            inv_two_ref[...])
    backward_rows(grad_ref[...], mixed_ref, vec_ref, kept, output_w, expand_w, shrink_w,
                  grad_mixed_ref, grad_one_ref, grad_output, grad_expand, grad_shrink, sums)

    @pl.when(pl.program_id(0) == pl.num_programs(0) - 1)
    def _():
        pack_second(offsets, place_ref[0], slots_ref, grad_output, grad_expand, grad_shrink)


def dense_turn_kernel(offsets, place_ref, live_ref, weight_ref, x_ref, mixed_ref, near_ref, far_ref,
                      vec_ref, cot_ref, result_ref, grad_mixed_ref, grad_one_ref, slots_ref, sums,
                      output_w, expand_w, shrink_w, grad_output, grad_expand, grad_shrink):
    step = pl.program_id(0)

    @pl.when(step == 0)
    def _():
        unpack_second(offsets, place_ref[0], near_ref, far_ref, output_w, expand_w, shrink_w)
        for item in (sums, grad_output, grad_expand, grad_shrink):
            item[...] = jnp.zeros_like(item)

    *kept, result = forward_rows(x_ref, mixed_ref, vec_ref, output_w, expand_w, shrink_w)
    result_ref[...] = result.astype(HALF)
    rows = cot_ref.shape[0]
    slot = lax.broadcasted_iota(jnp.int32, (rows, 1), 0) + step * rows
    grad_rows = cot_ref[...].astype(FLOAT) * jnp.where(slot < live_ref[0], weight_ref[0], 0.0)
    backward_rows(grad_rows, mixed_ref, vec_ref, kept, output_w, expand_w, shrink_w,
                  grad_mixed_ref, grad_one_ref, grad_output, grad_expand, grad_shrink, sums)

    @pl.when(step == pl.num_programs(0) - 1)
    def _():
        pack_second(offsets, place_ref[0], slots_ref, grad_output, grad_expand, grad_shrink)


def by_rows(width):
    return pl.BlockSpec((ROW_BLOCK, width), lambda i, *p: (i, 0))


def fixed(*shape):
    return pl.BlockSpec(shape, lambda i, *p: (0,) * len(shape))


def dense_call(offsets, place, x, mixed, near, far, vectors):
    rows, width = x.shape
    like = jax.ShapeDtypeStruct
    return pl.pallas_call(
        functools.partial(dense_kernel, offsets),
        grid_spec=pltpu.PrefetchScalarGridSpec(
            num_scalar_prefetch=1,
            grid=(rows // ROW_BLOCK,),
            in_specs=[by_rows(width), by_rows(width), fixed(*near.shape), fixed(*far.shape),
                      fixed(16, width)],
            out_specs=[by_rows(width), by_rows(width), by_rows(1), by_rows(2 * width),
                       by_rows(2 * width), by_rows(width), by_rows(1), fixed(width, width),
                       fixed(width, 2 * width), fixed(2 * width, width)],
        ),
        out_shape=[like((rows, width), HALF), like((rows, width), FLOAT), like((rows, 1), FLOAT),
                   like((rows, 2 * width), HALF), like((rows, 2 * width), FLOAT),
                   like((rows, width), FLOAT), like((rows, 1), FLOAT), like((width, width), HALF),
                   like((width, 2 * width), HALF), like((2 * width, width), HALF)],
        compiler_params=pltpu.CompilerParams(vmem_limit_bytes=VMEM_LIMIT),
        cost_estimate=pl.CostEstimate(
            flops=10 * rows * width * width, bytes_accessed=16 * 1024 * 1024,
            transcendentals=4 * rows * width,
        ),
        name="dense",
    )(place, x, mixed, near, far, vectors)


def dense_back_call(offsets, place, grad_rows, mixed, vectors, kept, weights):
    rows, width = grad_rows.shape
    like = jax.ShapeDtypeStruct
    return pl.pallas_call(
        functools.partial(dense_back_kernel, offsets),
        grid_spec=pltpu.PrefetchScalarGridSpec(
            num_scalar_prefetch=1,
            grid=(rows // ROW_BLOCK,),
            in_specs=[by_rows(width), by_rows(width), fixed(16, width), by_rows(width), by_rows(1),
                      by_rows(2 * width), by_rows(2 * width), by_rows(width), by_rows(1),
                      fixed(width, width), fixed(width, 2 * width), fixed(2 * width, width)],
            out_specs=[by_rows(width), by_rows(width), fixed(32, 80, width), fixed(16, width)],
            scratch_shapes=[pltpu.VMEM((width, width), FLOAT), pltpu.VMEM((width, 2 * width), FLOAT),
                            pltpu.VMEM((2 * width, width), FLOAT)],
        ),
        out_shape=[like((rows, width), HALF), like((rows, width), FLOAT),
                   like((32, 80, width), HALF), like((16, width), FLOAT)],
        compiler_params=pltpu.CompilerParams(vmem_limit_bytes=VMEM_LIMIT),
        cost_estimate=pl.CostEstimate(
            flops=20 * rows * width * width, bytes_accessed=20 * 1024 * 1024, transcendentals=0
        ),
        name="dense_back",
    )(place, grad_rows, mixed, vectors, *kept, *weights)


def dense_turn_call(offsets, place, live, weight, x, mixed, near, far, vectors, cotangent):
    rows, width = x.shape
    like = jax.ShapeDtypeStruct
    return pl.pallas_call(
        functools.partial(dense_turn_kernel, offsets),
        grid_spec=pltpu.PrefetchScalarGridSpec(
            num_scalar_prefetch=3,
            grid=(rows // ROW_BLOCK,),
            in_specs=[by_rows(width), by_rows(width), fixed(*near.shape), fixed(*far.shape),
                      fixed(16, width), by_rows(width)],
            out_specs=[by_rows(width), by_rows(width), by_rows(width), fixed(32, 80, width),
                       fixed(16, width)],
            scratch_shapes=[pltpu.VMEM((width, width), HALF), pltpu.VMEM((width, 2 * width), HALF),
                            pltpu.VMEM((2 * width, width), HALF),
                            pltpu.VMEM((width, width), FLOAT), pltpu.VMEM((width, 2 * width), FLOAT),
                            pltpu.VMEM((2 * width, width), FLOAT)],
        ),
        out_shape=[like((rows, width), HALF), like((rows, width), HALF), like((rows, width), FLOAT),
                   like((32, 80, width), HALF), like((16, width), FLOAT)],
        compiler_params=pltpu.CompilerParams(vmem_limit_bytes=VMEM_LIMIT),
        cost_estimate=pl.CostEstimate(
            flops=30 * rows * width * width, bytes_accessed=16 * 1024 * 1024,
            transcendentals=4 * rows * width,
        ),
        name="dense_turn",
    )(place, live, weight, x, mixed, near, far, vectors, cotangent)


def attend_back_kernel(offsets, place_ref, x_ref, joint_ref, probs_ref, grad_mixed_ref, weight_ref,
                       grad_one_ref, slots_ref, grad_x_ref, sums_ref, x_turned, grad_scores,
                       grad_joint):
    head = pl.program_id(0)
    rows = x_ref.shape[0]
    head_size = grad_mixed_ref.shape[1]
    place = place_ref[0]

    @pl.when(head == 0)
    def _():
        x_turned[...] = jnp.transpose(x_ref[...])
        grad_x_ref[...] = grad_one_ref[...]
        grad_joint[CTX:, head_size:] = jnp.zeros((rows - CTX, 2 * head_size), HALF)

    keys = joint_ref[0, :CTX, head_size : 2 * head_size]
    values = joint_ref[0, :CTX, 2 * head_size :]
    keys_turned = jnp.transpose(keys)
    factor = head_size ** (-0.5)
    for start in range(0, rows, SCORE_BLOCK):
        span = slice(start, start + SCORE_BLOCK)
        grad_probs = product(values, grad_mixed_ref[span, :], 1, 1)
        probs = probs_ref[0, :, span].astype(FLOAT)
        weighted = probs * grad_probs
        grad_low = (factor * (weighted - probs * column_sum(weighted))).astype(HALF)
        grad_scores[:, span] = grad_low
        grad_joint[span, :head_size] = jnp.transpose(product(keys_turned, grad_low, 1, 0)).astype(
            HALF
        )
    grad_joint[:CTX, head_size : 2 * head_size] = product(
        grad_scores[...], joint_ref[0, :, :head_size], 1, 0
    ).astype(HALF)
    grad_joint[:CTX, 2 * head_size :] = product(probs_ref[0], grad_mixed_ref[...], 1, 0).astype(HALF)
    sums = column_sum(grad_joint[...].astype(FLOAT))
    sums_ref[0:1, :] = sums[:, :head_size]
    sums_ref[1:2, :] = sums[:, 2 * head_size :]
    grad_weight = product(x_turned[...], grad_joint[...], 1, 0)
    grad_low = grad_weight.astype(HALF)
    grad_x_ref[...] += product(grad_joint[...], weight_ref[0], 1, 1)
    holder = grad_scores
    holder[: grad_low.shape[0], : 3 * head_size] = grad_low
    for at, offset in enumerate(offsets):
        span = owner_rows(offset, place, 16)
        for piece in range(3):
            slots_ref[at, piece * 16 : (piece + 1) * 16, :] = holder[
                span, piece * head_size : (piece + 1) * head_size
            ]


def attend_back_call(offsets, place, x, joint, probs, grad_mixed, weight, grad_one):
    rows, width = x.shape
    head_size = width // HEADS
    like = jax.ShapeDtypeStruct
    return pl.pallas_call(
        functools.partial(attend_back_kernel, offsets),
        grid_spec=pltpu.PrefetchScalarGridSpec(
            num_scalar_prefetch=1,
            grid=(HEADS,),
            in_specs=[
                pl.BlockSpec((rows, width), lambda h, p: (0, 0)),
                pl.BlockSpec((1, rows, 3 * head_size), lambda h, p: (h, 0, 0)),
                pl.BlockSpec((1, CTX, rows), lambda h, p: (h, 0, 0)),
                pl.BlockSpec((rows, head_size), lambda h, p: (0, h)),
                pl.BlockSpec((1, width, 3 * head_size), lambda h, p: (h, 0, 0)),
                pl.BlockSpec((rows, width), lambda h, p: (0, 0)),
            ],
            out_specs=[
                pl.BlockSpec((32, 48, head_size), lambda h, p: (0, 0, h)),
                pl.BlockSpec((rows, width), lambda h, p: (0, 0)),
                pl.BlockSpec((8, head_size), lambda h, p: (0, h)),
            ],
            scratch_shapes=[pltpu.VMEM((width, rows), HALF), pltpu.VMEM((CTX, rows), HALF),
                            pltpu.VMEM((rows, 3 * head_size), HALF)],
        ),
        out_shape=[like((32, 48, width), HALF), like((rows, width), FLOAT),
                   like((8, width), FLOAT)],
        compiler_params=pltpu.CompilerParams(vmem_limit_bytes=VMEM_LIMIT),
        cost_estimate=pl.CostEstimate(
            flops=12 * rows * width * width + 8 * rows * CTX * width,
            bytes_accessed=20 * 1024 * 1024, transcendentals=0,
        ),
        name="attend_back",
    )(place, x, joint, probs, grad_mixed, weight, grad_one)


class Route:
    def __init__(self, steps, inner_size):
        self.steps = steps
        masks = [bit * inner_size if axis == "dp" else bit for axis, size, bit in steps]
        self.count = 1 << len(steps)
        self.offset = [
            sum(mask for at, mask in enumerate(masks) if place >> at & 1)
            for place in range(self.count)
        ]

    def swap(self, at, payload):
        axis, size, bit = self.steps[at]
        return lax.ppermute(payload, axis, [(one, one ^ bit) for one in range(size)])


def routes(outer_size, inner_size):
    outer = [("dp", outer_size, 1 << at) for at in reversed(range(outer_size.bit_length() - 1))]
    inner = [("fsdp", inner_size, 1 << at) for at in reversed(range(inner_size.bit_length() - 1))]
    first = inner + outer
    second = inner[:-1] + outer[:-1] + inner[-1:] + outer[-1:]
    return (Route(first, inner_size), Route(second, inner_size))


def spread(route, block, shared=None):
    rows, width = block.shape
    last = len(route.steps) - 1
    for at in range(last + 1):
        held = block.shape[0]
        payload = block if shared is None else jnp.concatenate([block, shared])
        got = route.swap(at, payload)
        if shared is not None:
            shared = shared + got[held:]
        if at == last:
            far = got[:held].reshape(route.count // 2, rows, width)
            return (block.reshape(route.count // 2, rows, width), far, shared)
        block = jnp.concatenate([block, got[:held]])


def gather_sum(route, slots, shared=None):
    count, rows, width = slots.shape
    block = slots.reshape(count * rows, width)
    for at in reversed(range(len(route.steps))):
        half = block.shape[0] // 2
        payload = block[half:] if shared is None else jnp.concatenate([block[half:], shared])
        got = route.swap(at, payload)
        block = (block[:half].astype(FLOAT) + got[:half].astype(FLOAT)).astype(HALF)
        if shared is not None:
            shared = (shared.astype(FLOAT) + got[half:].astype(FLOAT)).astype(HALF)
    return (block, shared)


def split_parts(slots, parts):
    ends = np.cumsum((0,) + parts)
    return [slots[:, ends[at] : ends[at + 1]] for at in range(len(parts))]


def coarse(route, near, far, place, parts):
    position = np.zeros((route.count,), np.int32)
    for at, off in enumerate(route.offset):
        position[off] = at
    owners = jnp.arange(route.count, dtype=jnp.int32)
    slots = jnp.take(jnp.concatenate([near, far]), jnp.asarray(position)[owners ^ place], axis=0)
    fine = tuple(part * OWNERS // route.count for part in parts)
    slots = jnp.concatenate(
        [
            piece.reshape(OWNERS, part, piece.shape[2])
            for part, piece in zip(parts, split_parts(slots, fine), strict=True)
        ],
        axis=1,
    )
    return (slots[: OWNERS // 2], slots[OWNERS // 2 :])


def fine(route, slots, place, parts):
    each = [part * OWNERS // route.count for part in parts]
    slots = jnp.concatenate(
        [
            piece.reshape(route.count, rows, piece.shape[2])
            for rows, piece in zip(each, split_parts(slots, parts), strict=True)
        ],
        axis=1,
    )
    return jnp.take(slots, jnp.asarray(route.offset, jnp.int32) ^ place, axis=0)


def wide_to_rows(shard, width):
    return jnp.concatenate(
        [shard[:, at * width : (at + 1) * width] for at in range(shard.shape[1] // width)]
    )


def rows_to_wide(rows, pieces):
    each = rows.shape[0] // pieces
    return jnp.concatenate([rows[at * each : (at + 1) * each] for at in range(pieces)], axis=1)


def advance(master, moment, average, grad, momentum, step_rate, decay_now):
    new_moment = momentum * moment + grad
    new_master = master - step_rate * (grad + momentum * new_moment)
    new_average = decay_now * average + (1.0 - decay_now) * new_master
    return (new_moment, new_average, new_master, new_master.astype(jnp.bfloat16))


def shards(
    tokens,
    cotangent,
    dataset_ids,
    query_counts,
    learn_rate,
    momentum_coef,
    average_decay,
    step_count,
    attend_weight,
    attend_momentum,
    attend_average,
    output_weight,
    output_momentum,
    output_average,
    expand_weight,
    expand_momentum,
    expand_average,
    shrink_weight,
    shrink_momentum,
    shrink_average,
    norm_gains,
    gains_momentum,
    gains_average,
    bias_rows,
    bias_momentum,
    bias_average,
):
    masters = (attend_weight, output_weight, expand_weight, shrink_weight, norm_gains, bias_rows)
    moments = (
        attend_momentum,
        output_momentum,
        expand_momentum,
        shrink_momentum,
        gains_momentum,
        bias_momentum,
    )
    averages = (
        attend_average,
        output_average,
        expand_average,
        shrink_average,
        gains_average,
        bias_average,
    )
    layers = attend_weight.shape[0]
    width = attend_weight.shape[2] // 3
    each = attend_weight.shape[1]
    outer_size = lax.axis_size("dp")
    inner_size = lax.axis_size("fsdp")
    everyone = outer_size * inner_size
    place = lax.axis_index("dp") * inner_size + lax.axis_index("fsdp")
    first_route, second_route = routes(outer_size, inner_size)
    direct = everyone == OWNERS
    plain = tuple(range(OWNERS))
    first_order = tuple(first_route.offset) if direct else plain
    second_order = tuple(second_route.offset) if direct else plain
    where = (place if direct else jnp.zeros_like(place)).astype(jnp.int32).reshape(1)
    low = lambda item: item.astype(HALF)

    onehot = (dataset_ids[:, None] == jnp.arange(NDS, dtype=jnp.int32)[None, :]).astype(FLOAT)
    own = jnp.concatenate(
        [low(item[at]) for at in range(layers) for item in (norm_gains, bias_rows)]
    )
    shared = lax.dynamic_update_slice(
        jnp.zeros((24, width), HALF), own, (0, place * own.shape[1])
    )
    shared = shared.at[20, :NDS].set(low(jnp.sum(onehot, axis=0)))

    weights = []
    for at in range(layers):
        first = wide_to_rows(low(attend_weight[at]), width)
        second = jnp.concatenate(
            [
                low(output_weight[at]),
                wide_to_rows(low(expand_weight[at]), width),
                low(shrink_weight[at]),
            ]
        )
        if at == 0:
            first_near, first_far, shared = spread(first_route, first, shared)
        else:
            first_near, first_far, _ = spread(first_route, first)
        second_near, second_far, _ = spread(second_route, second)
        if not direct:
            first_near, first_far = coarse(first_route, first_near, first_far, place, FIRST_PARTS)
            second_near, second_far = coarse(
                second_route, second_near, second_far, place, SECOND_PARTS
            )
        weights.append((first_near, first_far, second_near, second_far))
    shared = shared.astype(FLOAT)
    vectors = [jnp.pad(shared[10 * at : 10 * at + 10], ((0, 6), (0, 0))) for at in range(layers)]
    counts = shared[20, :NDS]
    own_count = jnp.sum(onehot * counts[None, :], axis=1)
    row_weight = jnp.sum(counts) / (NDS * own_count)

    current = tokens[0]
    kept = []
    for at in range(layers):
        first_near, first_far, second_near, second_far = weights[at]
        joint, probs, mixed, attend_w = attend_call(
            first_order, where, current, first_near, first_far, vectors[at]
        )
        kept.append([current, joint, probs, mixed, attend_w])
        if at + 1 < layers:
            current, *rest = dense_call(
                second_order, where, current, mixed, second_near, second_far, vectors[at]
            )
            kept[at].extend([rest[:6], rest[6:]])
    shard_grads = [None] * layers
    for at in reversed(range(layers)):
        start, joint, probs, mixed, attend_w = kept[at][:5]
        if at + 1 == layers:
            result, grad_mixed, grad_one, second_slots, sums = dense_turn_call(
                second_order,
                where,
                query_counts + CTX,
                row_weight,
                start,
                mixed,
                weights[at][2],
                weights[at][3],
                vectors[at],
                cotangent[0],
            )
        else:
            grad_mixed, grad_one, second_slots, sums = dense_back_call(
                second_order, where, grad_rows, mixed, vectors[at], kept[at][5], kept[at][6]
            )
        first_slots, grad_rows, joint_sums = attend_back_call(
            first_order, where, start, joint, probs, grad_mixed, attend_w, grad_one
        )
        if not direct:
            second_slots = fine(second_route, second_slots, place, SECOND_PARTS)
            first_slots = fine(first_route, first_slots, place, FIRST_PARTS)
        second_sum, _ = gather_sum(second_route, second_slots)
        small = low(jnp.concatenate([sums[:2], joint_sums[:2], sums[4:]]))
        first_sum, small_sum = gather_sum(first_route, first_slots, small)
        own_small = lax.dynamic_slice(small_sum, (0, place * each), (10, each)).astype(FLOAT)
        shard_grads[at] = (
            rows_to_wide(first_sum, 3).astype(FLOAT),
            second_sum[:each].astype(FLOAT),
            rows_to_wide(second_sum[each : 3 * each], 2).astype(FLOAT),
            second_sum[3 * each :].astype(FLOAT),
            own_small[:2],
            own_small[2:],
        )
    step_value = step_count[0].astype(jnp.float32)
    decay_now = average_decay[0] * (1.0 + step_value) / (4.0 + step_value)
    outputs = [result[None], grad_rows[None]]
    for group_index in range(6):
        stacked = jnp.stack(
            [shard_grads[at][group_index] for at in range(layers)]
        )
        outputs.extend(
            advance(
                masters[group_index],
                moments[group_index],
                averages[group_index],
                stacked,
                momentum_coef[0],
                learn_rate[0],
                decay_now,
            )
        )
    return tuple(outputs)


def solution(mesh):
    return jax.shard_map(
        shards,
        mesh=mesh,
        in_specs=(
            P(("dp", "fsdp"), None, None),
            P(("dp", "fsdp"), None, None),
            P(("dp", "fsdp")),
            P(("dp", "fsdp")),
            P(),
            P(),
            P(),
            P(),
            P(None, ("dp", "fsdp"), None),
            P(None, ("dp", "fsdp"), None),
            P(None, ("dp", "fsdp"), None),
            P(None, ("dp", "fsdp"), None),
            P(None, ("dp", "fsdp"), None),
            P(None, ("dp", "fsdp"), None),
            P(None, ("dp", "fsdp"), None),
            P(None, ("dp", "fsdp"), None),
            P(None, ("dp", "fsdp"), None),
            P(None, ("dp", "fsdp"), None),
            P(None, ("dp", "fsdp"), None),
            P(None, ("dp", "fsdp"), None),
            P(None, None, ("dp", "fsdp")),
            P(None, None, ("dp", "fsdp")),
            P(None, None, ("dp", "fsdp")),
            P(None, None, ("dp", "fsdp")),
            P(None, None, ("dp", "fsdp")),
            P(None, None, ("dp", "fsdp")),
        ),
        out_specs=(
            P(("dp", "fsdp"), None, None),
            P(("dp", "fsdp"), None, None),
            P(None, ("dp", "fsdp"), None),
            P(None, ("dp", "fsdp"), None),
            P(None, ("dp", "fsdp"), None),
            P(None, ("dp", "fsdp"), None),
            P(None, ("dp", "fsdp"), None),
            P(None, ("dp", "fsdp"), None),
            P(None, ("dp", "fsdp"), None),
            P(None, ("dp", "fsdp"), None),
            P(None, ("dp", "fsdp"), None),
            P(None, ("dp", "fsdp"), None),
            P(None, ("dp", "fsdp"), None),
            P(None, ("dp", "fsdp"), None),
            P(None, ("dp", "fsdp"), None),
            P(None, ("dp", "fsdp"), None),
            P(None, ("dp", "fsdp"), None),
            P(None, ("dp", "fsdp"), None),
            P(None, None, ("dp", "fsdp")),
            P(None, None, ("dp", "fsdp")),
            P(None, None, ("dp", "fsdp")),
            P(None, None, ("dp", "fsdp")),
            P(None, None, ("dp", "fsdp")),
            P(None, None, ("dp", "fsdp")),
            P(None, None, ("dp", "fsdp")),
            P(None, None, ("dp", "fsdp")),
        ),
        check_vma=False,
    )
```

time: 485 us -> 300 us (0.62); the launches traced: 479 us -> 299 us
  Pallas kernels: 0 us -> 131 us
  matrix products: 129 us -> 0 us
  local copies, waits for them, and re-layouts: 148 us -> 29.9 us
  other arithmetic: 94.5 us -> 17.1 us
  waiting for transfers between devices: 55.3 us -> 65.8 us
    pallas_call x0 -> x7, Pallas kernels: none -> 131 us  [the longest x2 49.8 us: attend_back_call(): pl.pallas_call(functools.partial(attend_back_kernel, offsets), grid_spec=...]
    dot_general x36 -> x0, matrix products: 129 us -> none  [the longest x2 22.2 us: layer_forward(): jnp.dot(first_low, expand_w, preferred_element_type=jnp.float32)]
    unnamed x292 -> x97, local copies, waits for them, and re-layouts: 47.9 us -> 18.6 us
    gather x10 -> x0, local copies, waits for them, and re-layouts: 26.9 us -> none  [the longest x4 15 us: by_position(): return jnp.take(slots, jnp.asarray(route.offset, jnp.int32) ^ place, axis=0)]
    reduce_sum x13 -> x0, other arithmetic: 26 us -> none  [the longest x2 15.2 us: attend_one(): jnp.sum(jnp.exp(scaled - row_top), axis=-1, keepdims=True)]
    convert_element_type x36 -> x32, other arithmetic: 27.7 us -> 2.77 us  [the longest x20 2.51 us: gather_sum(): block = (block[:half].astype(FLOAT) + got[:half].astype(FLOAT)).astype(HALF)]
    reshape x8 -> x0, local copies, waits for them, and re-layouts: 20.5 us -> none  [the longest x6 20.4 us: wide_to_slots(): grad.reshape(owners, rows // owners, pieces, width).transpose(0, 2, 1, 3)]
    transpose x6 -> x0, local copies, waits for them, and re-layouts: 11.9 us -> none  [the longest x2 6.65 us: wide_to_slots(): return grad.reshape(owners, rows // owners, pieces, width).transpose(0, 2...]
  transfers between devices with their start and end apart: 40 -> 40, of which waited for: 16 -> 19; matrix products, arithmetic and copies ran while one was open for 31% -> 11% of each run, Pallas kernels for 0% -> 16%
where the time goes in v2:
time: 300 us; the launch traced here: 299 us
  Pallas kernels  131 us (44%)
  waiting for transfers between devices  65.8 us (22%)
  starting transfers between devices  48.7 us (16%)
  local copies, waits for them, and re-layouts  29.9 us (10%)
  other arithmetic  17.1 us (6%)
  between operations  6.8 us (2%)
    ppermute x40, waiting for transfers between devices, swap(): lax.ppermute(payload, axis, [(one, one ^ bit) for one in range(size)])  65.8 us
    pallas_call x2, Pallas kernels, attend_back_call(): pl.pallas_call(functools.partial(attend_back_kernel, offsets), grid_spec=...  49.8 us
    ppermute x40, starting transfers between devices, swap(): lax.ppermute(payload, axis, [(one, one ^ bit) for one in range(size)])  48.7 us
    pallas_call x2, Pallas kernels, attend_call(): pl.pallas_call(functools.partial(attend_kernel, offsets), grid_spec=pltpu...  37.6 us
    pallas_call x1, Pallas kernels, dense_turn_call(): pl.pallas_call(functools.partial(dense_turn_kernel, offsets), grid_spec=p...  18.8 us
    unnamed x97, local copies, waits for them, and re-layouts  18.6 us
    pallas_call x1, Pallas kernels, dense_back_call(): pl.pallas_call(functools.partial(dense_back_kernel, offsets), grid_spec=p...  14.7 us
    pallas_call x1, Pallas kernels, dense_call(): pl.pallas_call(functools.partial(dense_kernel, offsets), grid_spec=pltpu....  10.2 us
  transfers between devices with their start and end apart: 40, of which 19 were waited for; matrix products, arithmetic and copies ran while one was open for 11% of the time, Pallas kernels for 16%

profile of v2, /device:TPU:0, one launch (start us, length us, event | category | flops | bytes accessed | tf_op | source)
XLA Modules:
  0.0 299.4 jit_solution(14138925196513791030)
XLA Ops:
  6.0 4.1 %collective-permute-start.15 = (bf16[80,512]{1,0:T(8,128)(2,1)S(1)}, bf16[80,512]{1,0:T(8,128)(2,1)S(1)}, u32[]{:S(2)}, u32[]{:S(2)}) collective-permute-start(bf16[80,512]{1,0:T(8,128)(2,1)S(1)} %pad_maximum_fusion.10), channel_id=1, source_target_pairs={{0,4},{1,5},{2,6},{3,7},{4,0},{5,1},{6,2},{7,3},{8,12},{9,13},{10,... | collective-permute-start | bytes 245768 | tf_op jit(solution)/shard_map/ppermute | solution.py:440
  13.3 2.9 collective-permute-start.5
  22.3 2.8 collective-permute-done
  28.6 3.3 %collective-permute-done.1 = bf16[120,512]{1,0:T(8,128)(2,1)S(1)} collective-permute-done((bf16[120,512]{1,0:T(8,128)(2,1)S(1)}, bf16[120,512]{1,0:T(8,128)(2,1)S(1)}, u32[]{:S(2)}, u32[]{:S(2)}) %collective-permute-start.1) | collective-permute-done | bytes 122912 | tf_op jit(solution)/shard_map/ppermute | solution.py:440
  46.1 2.2 collective-permute-done.7
  50.5 4.8 %collective-permute-done.3 = bf16[408,512]{1,0:T(8,128)(2,1)S(1)} collective-permute-done((bf16[408,512]{1,0:T(8,128)(2,1)}, bf16[408,512]{1,0:T(8,128)(2,1)S(1)}, u32[]{:S(2)}, u32[]{:S(2)}) %collective-permute-start.3) | collective-permute-done | bytes 417824 | tf_op jit(solution)/shard_map/ppermute | solution.py:440
  67.8 3.7 %collective-permute-done.13 = bf16[384,512]{1,0:T(8,128)(2,1)S(1)} collective-permute-done((bf16[384,512]{1,0:T(8,128)(2,1)}, bf16[384,512]{1,0:T(8,128)(2,1)S(1)}, u32[]{:S(2)}, u32[]{:S(2)}) %collective-permute-start.13) | collective-permute-done | bytes 393248 | tf_op jit(solution)/shard_map/ppermute | solution.py:440
  71.6 3.5 %collective-permute-done.18 = bf16[640,512]{1,0:T(8,128)(2,1)S(1)} collective-permute-done((bf16[640,512]{1,0:T(8,128)(2,1)}, bf16[640,512]{1,0:T(8,128)(2,1)S(1)}, u32[]{:S(2)}, u32[]{:S(2)}) %collective-permute-start.18) | collective-permute-done | bytes 655392 | tf_op jit(solution)/shard_map/ppermute | solution.py:440
  80.2 18.8 %attend.2 = (bf16[4,1024,384]{2,1,0:T(8,128)(2,1)}, bf16[4,896,1024]{2,1,0:T(8,128)(2,1)}, bf16[1024,512]{1,0:T(8,128)(2,1)}, bf16[4,512,384]{2,1,0:T(8,128)(2,1)}) custom-call(s32[1]{0:T(128)} %bitcast.place_ref, bf16[1024,512]{1,0:T(8,128)(2,1)} %bitcast.149, bf16[16,48,512]{2,1,0:T(8,128)(2,1)} %bitcast.146, bf16[16,48,512]{2,1,0:T(8,128)(2,1)} %bitcast.144, ...), custom_call_target="tpu_custom_call" | custom-call | flops 3489660928 | bytes 16777216 | tf_op jit(solution)/shard_map/attend/pallas_call | solution.py:75
  99.0 10.2 %dense.1 = (bf16[1024,512]{1,0:T(8,128)(2,1)}, f32[1024,512]{1,0:T(8,128)}, f32[1024,1]{1,0:T(8,128)}, bf16[1024,1024]{1,0:T(8,128)(2,1)}, f32[1024,1024]{1,0:T(...) custom-call(s32[1]{0:T(128)} %bitcast.place_ref, ...), custom_call_target="tpu_custom_call" | custom-call | flops 2684354560 | bytes 16777216 | tf_op jit(solution)/shard_map/dense/pallas_call | solution.py:267
  109.2 18.8 %attend.3 = (bf16[4,1024,384]{2,1,0:T(8,128)(2,1)}, bf16[4,896,1024]{2,1,0:T(8,128)(2,1)}, bf16[1024,512]{1,0:T(8,128)(2,1)}, bf16[4,512,384]{2,1,0:T(8,128)(2,1)}) custom-call(s32[1]{0:T(128)} %bitcast.place_ref, bf16[1024,512]{1,0:T(8,128)(2,1)} %get-tuple-element.72.x_ref, bf16[16,48,512]{2,1,0:T(8,128)(2,1)} %bitcast.145, ...), custom_call_target="tpu_custom_call" | custom-call | flops 3489660928 | bytes 16777216 | tf_op jit(solution)/shard_map/attend/pallas_call | solution.py:75
  128.0 18.8 %dense_turn.1 = (bf16[1024,512]{1,0:T(8,128)(2,1)}, bf16[1024,512]{1,0:T(8,128)(2,1)}, f32[1024,512]{1,0:T(8,128)}, bf16[32,80,512]{2,1,0:T(8,128)(2,1)}, f32[16,512]{1,0:T(8,128)}) custom-call(s32[1]{0:T(128)} %bitcast.place_ref, s32[1]{0:T(128)S(6)} %add.179.live_ref, f32[1]{0:T(128)} %bitcast.7.weight_ref, bf16[1024,512]{1,0:T(8,128)(2,1)} %get-tuple-element.72.x_ref, ...), custom_call_target="tpu_custom_call" | custom-call | flops 8053063680 | bytes 16777216 | tf_op jit(solution)/shard_map/dense_turn/pallas_call | solution.py:319
  146.8 24.8 %attend_back.2 = (bf16[32,48,512]{2,1,0:T(8,128)(2,1)}, f32[1024,512]{1,0:T(8,128)}, f32[8,512]{1,0:T(8,128)}) custom-call(s32[1]{0:T(128)} %bitcast.place_ref, bf16[1024,512]{1,0:T(8,128)(2,1)} %get-tuple-element.72.x_ref, bf16[4,1024,384]{2,1,0:T(8,128)(2,1)} %get-tuple-element.77.joint_ref, bf16[4,896,1024]{2,1,0:T(8,128)(2,1)} %get-tuple-element.78.probs_ref, ...), custom_call_target="tpu_custom_call" | custom-call | flops 6979321856 | bytes 20971520 | tf_op jit(solution)/shard_map/attend_back/pallas_call | solution.py:396
  171.6 14.7 %dense_back.1 = (bf16[1024,512]{1,0:T(8,128)(2,1)}, f32[1024,512]{1,0:T(8,128)}, bf16[32,80,512]{2,1,0:T(8,128)(2,1)}, f32[16,512]{1,0:T(8,128)}) custom-call(s32[1]{0:T(128)} %bitcast.place_ref, f32[1024,512]{1,0:T(8,128)} %get-tuple-element.82.grad_ref, bf16[1024,512]{1,0:T(8,128)(2,1)} %get-tuple-element.71.mixed_ref, ...), custom_call_target="tpu_custom_call" | custom-call | flops 5368709120 | bytes 20971520 | tf_op jit(solution)/shard_map/dense_back/pallas_call | solution.py:294
  187.1 25.0 %attend_back.3 = (bf16[32,48,512]{2,1,0:T(8,128)(2,1)}, f32[1024,512]{1,0:T(8,128)}, f32[8,512]{1,0:T(8,128)}) custom-call(s32[1]{0:T(128)} %bitcast.place_ref, bf16[1024,512]{1,0:T(8,128)(2,1)} %bitcast.151, bf16[4,1024,384]{2,1,0:T(8,128)(2,1)} %get-tuple-element.75.joint_ref, bf16[4,896,1024]{2,1,0:T(8,128)(2,1)} %get-tuple-element.76.probs_ref, ...), custom_call_target="tpu_custom_call" | custom-call | flops 6979321856 | bytes 20971520 | tf_op jit(solution)/shard_map/attend_back/pallas_call | solution.py:396
  222.2 9.9 %collective-permute-done.21 = bf16[400,512]{1,0:T(8,128)(2,1)S(1)} collective-permute-done((bf16[400,512]{1,0:T(8,128)(2,1)S(1)}, bf16[400,512]{1,0:T(8,128)(2,1)S(1)}, u32[]{:S(2)}, u32[]{:S(2)}) %collective-permute-start.21) | collective-permute-done | bytes 409632 | tf_op jit(solution)/shard_map/ppermute | solution.py:440
  233.8 6.5 %collective-permute-done.26 = bf16[400,512]{1,0:T(8,128)(2,1)S(1)} collective-permute-done((bf16[400,512]{1,0:T(8,128)(2,1)S(1)}, bf16[400,512]{1,0:T(8,128)(2,1)S(1)}, u32[]{:S(2)}, u32[]{:S(2)}) %collective-permute-start.26) | collective-permute-done | bytes 409632 | tf_op jit(solution)/shard_map/ppermute | solution.py:440
  246.5 2.2 collective-permute-done.27
  251.3 3.2 %collective-permute-start.24 = (bf16[64,512]{1,0:T(8,128)(2,1)S(1)}, bf16[64,512]{1,0:T(8,128)(2,1)S(1)}, u32[]{:S(2)}, u32[]{:S(2)}) collective-permute-start(bf16[64,512]{1,0:T(8,128)(2,1)S(1)} %pad_maximum_fusion.12), channel_id=1, source_target_pairs={{0,4},{1,5},{2,6},{3,7},{4,0},{5,1},{6,2},{7,3},{8,12},{9,13},{10,... | collective-permute-start | bytes 196616 | tf_op jit(solution)/shard_map/ppermute | solution.py:440
  254.5 2.3 collective-permute-start.29
  265.1 10.2 %collective-permute-done.36 = bf16[640,512]{1,0:T(8,128)(2,1)S(1)} collective-permute-done((bf16[640,512]{1,0:T(8,128)(2,1)S(1)}, bf16[640,512]{1,0:T(8,128)(2,1)S(1)}, u32[]{:S(2)}, u32[]{:S(2)}) %collective-permute-start.36) | collective-permute-done | bytes 655392 | tf_op jit(solution)/shard_map/ppermute | solution.py:440
  278.9 5.0 %collective-permute-done.37 = bf16[320,512]{1,0:T(8,128)(2,1)S(1)} collective-permute-done((bf16[320,512]{1,0:T(8,128)(2,1)S(1)}, bf16[320,512]{1,0:T(8,128)(2,1)S(1)}, u32[]{:S(2)}, u32[]{:S(2)}) %collective-permute-start.37) | collective-permute-done | bytes 327712 | tf_op jit(solution)/shard_map/ppermute | solution.py:440
  285.3 3.3 %collective-permute-start.34 = (bf16[80,512]{1,0:T(8,128)(2,1)S(1)}, bf16[80,512]{1,0:T(8,128)(2,1)S(1)}, u32[]{:S(2)}, u32[]{:S(2)}) collective-permute-start(bf16[80,512]{1,0:T(8,128)(2,1)S(1)} %slice.628), channel_id=1, source_target_pairs={{0,4},{1,5},{2,6},{3,7},{4,0},{5,1},{6,2},{7,3},{8,12},{9,13},{10,... | collective-permute-start | bytes 245768 | tf_op jit(solution)/shard_map/ppermute | solution.py:440
  289.8 2.7 collective-permute-start.39
  (291 shorter events, 88.8 us)
Async XLA Ops:
  6.0 28.3 %collective-permute-start.15 = (bf16[80,512]{1,0:T(8,128)(2,1)S(1)}, bf16[80,512]{1,0:T(8,128)(2,1)S(1)}, u32[]{:S(2)}, u32[]{:S(2)}) collective-permute-start(bf16[80,512]{1,0:T(8,128)(2,1)S(1)} %pad_maximum_fusion.10), channel_id=1, source_target_pairs={{0,4},{1,5},{2,6},{3,7},{4,0},{5,1},{6,2},{7,3},{8,12},{9,13},{10,... | collective-permute-start | bytes 245768 | tf_op jit(solution)/shard_map/ppermute | solution.py:440
  13.2 12.6 %collective-permute-start.10 = (bf16[48,512]{1,0:T(8,128)(2,1)S(1)}, bf16[48,512]{1,0:T(8,128)(2,1)S(1)}, u32[]{:S(2)}, u32[]{:S(2)}) collective-permute-start(bf16[48,512]{1,0:T(8,128)(2,1)S(1)} %pad_maximum_fusion.15), channel_id=1, source_target_pairs={{0,4},{1,5},{2,6},{3,7},{4,0},{5,1},{6,2},{7,3},{8,12},{9,13},{10,... | collective-permute-start | bytes 147464 | tf_op jit(solution)/shard_map/ppermute | solution.py:440
  13.3 14.6 %collective-permute-start.5 = (bf16[80,512]{1,0:T(8,128)(2,1)S(1)}, bf16[80,512]{1,0:T(8,128)(2,1)S(1)}, u32[]{:S(2)}, u32[]{:S(2)}) collective-permute-start(bf16[80,512]{1,0:T(8,128)(2,1)S(1)} %pad_maximum_fusion.9), channel_id=1, source_target_pairs={{0,4},{1,5},{2,6},{3,7},{4,0},{5,1},{6,2},{7,3},{8,12},{9,13},{10,... | collective-permute-start | bytes 245768 | tf_op jit(solution)/shard_map/ppermute | solution.py:440
  25.8 16.5 %collective-permute-start.11 = (bf16[96,512]{1,0:T(8,128)(2,1)S(1)}, bf16[96,512]{1,0:T(8,128)(2,1)S(1)}, u32[]{:S(2)}, u32[]{:S(2)}) collective-permute-start(bf16[96,512]{1,0:T(8,128)(2,1)S(1)} %pad_maximum_fusion.8), channel_id=1, source_target_pairs={{0,2},{1,3},{2,0},{3,1},{4,6},{5,7},{6,4},{7,5},{8,10},{9,11},{10,... | collective-permute-start | bytes 294920 | tf_op jit(solution)/shard_map/ppermute | solution.py:440
  35.0 9.5 %collective-permute-start.16 = (bf16[160,512]{1,0:T(8,128)(2,1)S(1)}, bf16[160,512]{1,0:T(8,128)(2,1)S(1)}, u32[]{:S(2)}, u32[]{:S(2)}) collective-permute-start(bf16[160,512]{1,0:T(8,128)(2,1)S(1)} %get-tuple-element.169), channel_id=1, source_target_pairs={{0,2},{1,3},{2,0},{3,1},{4,6},{5,7},{6,4},{7,5},{8,10},{9,11},{10,... | collective-permute-start | bytes 491528 | tf_op jit(solution)/shard_map/ppermute | solution.py:440
  37.5 10.8 %collective-permute-start.7 = (bf16[320,512]{1,0:T(8,128)(2,1)}, bf16[320,512]{1,0:T(8,128)(2,1)S(1)}, u32[]{:S(2)}, u32[]{:S(2)}) collective-permute-start(bf16[320,512]{1,0:T(8,128)(2,1)} %get-tuple-element.150), channel_id=1, source_target_pairs={{0,16},{8,24},{16,0},{24,8},{1,17},{9,25},{17,1},{25,9},{2,18},{10... | collective-permute-start | bytes 983048 | tf_op jit(solution)/shard_map/ppermute | solution.py:440
  40.4 14.9 %collective-permute-start.3 = (bf16[408,512]{1,0:T(8,128)(2,1)}, bf16[408,512]{1,0:T(8,128)(2,1)S(1)}, u32[]{:S(2)}, u32[]{:S(2)}) collective-permute-start(bf16[408,512]{1,0:T(8,128)(2,1)} %constant_dynamic-update-slice_fusion.11), channel_id=1, source_target_pairs={{0,16},{8,24},{16,0},{24,8},{1,17},{9,25},{17,1},{25,9},{2,18},{10... | collective-permute-start | bytes 1253384 | tf_op jit(solution)/shard_map/ppermute | solution.py:440
  43.0 18.2 %collective-permute-start.12 = (bf16[192,512]{1,0:T(8,128)(2,1)S(1)}, bf16[192,512]{1,0:T(8,128)(2,1)S(1)}, u32[]{:S(2)}, u32[]{:S(2)}) collective-permute-start(bf16[192,512]{1,0:T(8,128)(2,1)S(1)} %get-tuple-element.157), channel_id=1, source_target_pairs={{0,1},{1,0},{2,3},{3,2},{4,5},{5,4},{6,7},{7,6},{8,9},{9,8},{10,11... | collective-permute-start | bytes 589832 | tf_op jit(solution)/shard_map/ppermute | solution.py:440
  45.3 13.6 %collective-permute-start.17 = (bf16[320,512]{1,0:T(8,128)(2,1)S(1)}, bf16[320,512]{1,0:T(8,128)(2,1)S(1)}, u32[]{:S(2)}, u32[]{:S(2)}) collective-permute-start(bf16[320,512]{1,0:T(8,128)(2,1)S(1)} %get-tuple-element.147), channel_id=1, source_target_pairs={{0,16},{8,24},{16,0},{24,8},{1,17},{9,25},{17,1},{25,9},{2,18},{10... | collective-permute-start | bytes 983048 | tf_op jit(solution)/shard_map/ppermute | solution.py:440
  49.0 14.5 %collective-permute-start.8 = (bf16[640,512]{1,0:T(8,128)(2,1)S(1)}, bf16[640,512]{1,0:T(8,128)(2,1)S(1)}, u32[]{:S(2)}, u32[]{:S(2)}) collective-permute-start(bf16[640,512]{1,0:T(8,128)(2,1)S(1)} %get-tuple-element.138), channel_id=1, source_target_pairs={{0,1},{1,0},{2,3},{3,2},{4,5},{5,4},{6,7},{7,6},{8,9},{9,8},{10,11... | collective-permute-start | bytes 1966088 | tf_op jit(solution)/shard_map/ppermute | solution.py:440
  56.8 19.2 %collective-permute-start.4 = (bf16[792,512]{1,0:T(8,128)(2,1)}, bf16[792,512]{1,0:T(8,128)(2,1)S(1)}, u32[]{:S(2)}, u32[]{:S(2)}) collective-permute-start(bf16[792,512]{1,0:T(8,128)(2,1)} %constant_dynamic-update-slice_fusion.18), channel_id=1, source_target_pairs={{0,8},{8,0},{16,24},{24,16},{1,9},{9,1},{17,25},{25,17},{2,10},{10... | collective-permute-start | bytes 2433032 | tf_op jit(solution)/shard_map/ppermute | solution.py:440
  59.8 15.3 %collective-permute-start.18 = (bf16[640,512]{1,0:T(8,128)(2,1)}, bf16[640,512]{1,0:T(8,128)(2,1)S(1)}, u32[]{:S(2)}, u32[]{:S(2)}) collective-permute-start(bf16[640,512]{1,0:T(8,128)(2,1)} %get-tuple-element.136), channel_id=1, source_target_pairs={{0,1},{1,0},{2,3},{3,2},{4,5},{5,4},{6,7},{7,6},{8,9},{9,8},{10,11... | collective-permute-start | bytes 1966088 | tf_op jit(solution)/shard_map/ppermute | solution.py:440
  62.0 9.4 %collective-permute-start.13 = (bf16[384,512]{1,0:T(8,128)(2,1)}, bf16[384,512]{1,0:T(8,128)(2,1)S(1)}, u32[]{:S(2)}, u32[]{:S(2)}) collective-permute-start(bf16[384,512]{1,0:T(8,128)(2,1)} %get-tuple-element.143), channel_id=1, source_target_pairs={{0,16},{8,24},{16,0},{24,8},{1,17},{9,25},{17,1},{25,9},{2,18},{10... | collective-permute-start | bytes 1179656 | tf_op jit(solution)/shard_map/ppermute | solution.py:440
  64.5 34.5 %collective-permute-start.9 = (bf16[1280,512]{1,0:T(8,128)(2,1)}, bf16[1280,512]{1,0:T(8,128)(2,1)}, u32[]{:S(2)}, u32[]{:S(2)}) collective-permute-start(bf16[1280,512]{1,0:T(8,128)(2,1)} %constant_dynamic-update-slice_fusion.49), channel_id=1, source_target_pairs={{0,8},{8,0},{16,24},{24,16},{1,9},{9,1},{17,25},{25,17},{2,10},{10... | collective-permute-start | bytes 3932168 | tf_op jit(solution)/shard_map/ppermute | solution.py:440
  71.5 37.7 %collective-permute-start.14 = (bf16[768,512]{1,0:T(8,128)(2,1)S(1)}, bf16[768,512]{1,0:T(8,128)(2,1)}, u32[]{:S(2)}, u32[]{:S(2)}) collective-permute-start(bf16[768,512]{1,0:T(8,128)(2,1)S(1)} %constant_dynamic-update-slice_fusion.68), channel_id=1, source_target_pairs={{0,8},{8,0},{16,24},{24,16},{1,9},{9,1},{17,25},{25,17},{2,10},{10... | collective-permute-start | bytes 2359304 | tf_op jit(solution)/shard_map/ppermute | solution.py:440
  76.0 52.0 %collective-permute-start.19 = (bf16[1280,512]{1,0:T(8,128)(2,1)}, bf16[1280,512]{1,0:T(8,128)(2,1)}, u32[]{:S(2)}, u32[]{:S(2)}) collective-permute-start(bf16[1280,512]{1,0:T(8,128)(2,1)} %constant_dynamic-update-slice_fusion.93), channel_id=1, source_target_pairs={{0,8},{8,0},{16,24},{24,16},{1,9},{9,1},{17,25},{25,17},{2,10},{10... | collective-permute-start | bytes 3932168 | tf_op jit(solution)/shard_map/ppermute | solution.py:440
  217.4 24.6 %collective-permute-start.30 = (bf16[1280,512]{1,0:T(8,128)(2,1)S(1)}, bf16[1280,512]{1,0:T(8,128)(2,1)S(1)}, u32[]{:S(2)}, u32[]{:S(2)}) collective-permute-start(bf16[1280,512]{1,0:T(8,128)(2,1)S(1)} %bitcast.143), channel_id=1, source_target_pairs={{0,8},{8,0},{16,24},{24,16},{1,9},{9,1},{17,25},{25,17},{2,10},{10... | collective-permute-start | bytes 3932168 | tf_op jit(solution)/shard_map/ppermute | solution.py:440
  219.2 24.0 %collective-permute-start.35 = (bf16[1280,512]{1,0:T(8,128)(2,1)S(1)}, bf16[1280,512]{1,0:T(8,128)(2,1)S(1)}, u32[]{:S(2)}, u32[]{:S(2)}) collective-permute-start(bf16[1280,512]{1,0:T(8,128)(2,1)S(1)} %bitcast.142), channel_id=1, source_target_pairs={{0,8},{8,0},{16,24},{24,16},{1,9},{9,1},{17,25},{25,17},{2,10},{10... | collective-permute-start | bytes 3932168 | tf_op jit(solution)/shard_map/ppermute | solution.py:440
  219.7 12.4 %collective-permute-start.21 = (bf16[400,512]{1,0:T(8,128)(2,1)S(1)}, bf16[400,512]{1,0:T(8,128)(2,1)S(1)}, u32[]{:S(2)}, u32[]{:S(2)}) collective-permute-start(bf16[400,512]{1,0:T(8,128)(2,1)S(1)} %pad_maximum_fusion.2), channel_id=1, source_target_pairs={{0,16},{8,24},{16,0},{24,8},{1,17},{9,25},{17,1},{25,9},{2,18},{10... | collective-permute-start | bytes 1228808 | tf_op jit(solution)/shard_map/ppermute | solution.py:440
  221.6 18.7 %collective-permute-start.26 = (bf16[400,512]{1,0:T(8,128)(2,1)S(1)}, bf16[400,512]{1,0:T(8,128)(2,1)S(1)}, u32[]{:S(2)}, u32[]{:S(2)}) collective-permute-start(bf16[400,512]{1,0:T(8,128)(2,1)S(1)} %pad_maximum_fusion.3), channel_id=1, source_target_pairs={{0,16},{8,24},{16,0},{24,8},{1,17},{9,25},{17,1},{25,9},{2,18},{10... | collective-permute-start | bytes 1228808 | tf_op jit(solution)/shard_map/ppermute | solution.py:440
  232.3 13.0 %collective-permute-start.22 = (bf16[208,512]{1,0:T(8,128)(2,1)S(1)}, bf16[208,512]{1,0:T(8,128)(2,1)S(1)}, u32[]{:S(2)}, u32[]{:S(2)}) collective-permute-start(bf16[208,512]{1,0:T(8,128)(2,1)S(1)} %pad_maximum_fusion.4), channel_id=1, source_target_pairs={{0,1},{1,0},{2,3},{3,2},{4,5},{5,4},{6,7},{7,6},{8,9},{9,8},{10,11... | collective-permute-start | bytes 638984 | tf_op jit(solution)/shard_map/ppermute | solution.py:440
  242.6 20.7 %collective-permute-start.31 = (bf16[640,512]{1,0:T(8,128)(2,1)S(1)}, bf16[640,512]{1,0:T(8,128)(2,1)S(1)}, u32[]{:S(2)}, u32[]{:S(2)}) collective-permute-start(bf16[640,512]{1,0:T(8,128)(2,1)S(1)} %slice.622), channel_id=1, source_target_pairs={{0,1},{1,0},{2,3},{3,2},{4,5},{5,4},{6,7},{7,6},{8,9},{9,8},{10,11... | collective-permute-start | bytes 1966088 | tf_op jit(solution)/shard_map/ppermute | solution.py:440
  243.7 31.7 %collective-permute-start.36 = (bf16[640,512]{1,0:T(8,128)(2,1)S(1)}, bf16[640,512]{1,0:T(8,128)(2,1)S(1)}, u32[]{:S(2)}, u32[]{:S(2)}) collective-permute-start(bf16[640,512]{1,0:T(8,128)(2,1)S(1)} %slice.631), channel_id=1, source_target_pairs={{0,1},{1,0},{2,3},{3,2},{4,5},{5,4},{6,7},{7,6},{8,9},{9,8},{10,11... | collective-permute-start | bytes 1966088 | tf_op jit(solution)/shard_map/ppermute | solution.py:440
  263.5 14.2 %collective-permute-start.32 = (bf16[320,512]{1,0:T(8,128)(2,1)S(1)}, bf16[320,512]{1,0:T(8,128)(2,1)S(1)}, u32[]{:S(2)}, u32[]{:S(2)}) collective-permute-start(bf16[320,512]{1,0:T(8,128)(2,1)S(1)} %slice.624), channel_id=1, source_target_pairs={{0,16},{8,24},{16,0},{24,8},{1,17},{9,25},{17,1},{25,9},{2,18},{10... | collective-permute-start | bytes 983048 | tf_op jit(solution)/shard_map/ppermute | solution.py:440
  (51 other events, 412.7 us)
